TPU v7x, 32 devices: a whole 2x2x4 slice. The times are simulated.
32 devices in a mesh: batch: 4 (over y, core), rows: 8 (over z, x).
Axes of the slice: x: 2, y: 2, z: 4, core: 2. Of those that a mesh axis runs over, the one named last changes fastest.
Arguments:
- features: float32 [4, 16384, 100], P('batch', 'rows'), may hold values from -6 to 6
- edge_rows: int32 [4, 8, 2, 16384], P('batch', 'rows'), may hold values from 0 to 3071, as said below
- edge_weight: float32 [4, 8, 16384], P('batch', 'rows'), may hold values from 0.02 to 0.2
- halo_counts: int32 [4, 8, 2], P('batch', 'rows'), may hold values from 1 to 512
- labels: int32 [4, 16384], P('batch', 'rows'), may hold values from 0 to 46
- pair_rows: int32 [4, 8, 8, 4], P('batch', 'rows'), may hold values from 0 to 2047
- step: int32 [1], replicated, may hold values from 2 to 20
- w_in: float32 [100, 256], P(None, 'batch'), may hold values from -0.625 to 0.625
- w_conv: float32 [3, 512, 256], P(None, 'batch'), may hold values from -0.25 to 0.25
- w_head: float32 [256, 47], P('batch'), may hold values from -0.375 to 0.375
- biases: float32 [4, 256], replicated, may hold values from -1 to 1
- norm_params: float32 [3, 2, 256], replicated, may hold values from 0.5 to 1.5
- head_bias: float32 [47], replicated, may hold values from -2 to 2
- mom_in: float32 [100, 256], P(None, 'batch'), may hold values from -0.0234375 to 0.0234375
- mom_conv: float32 [3, 512, 256], P(None, 'batch'), may hold values from -0.0234375 to 0.0234375
- mom_head: float32 [256, 47], P('batch'), may hold values from -0.0234375 to 0.0234375
- first_bias: float32 [4, 256], replicated, may hold values from -0.0024414062 to 0.0024414062
- first_norm: float32 [3, 2, 256], replicated, may hold values from -0.0024414062 to 0.0024414062
- first_head: float32 [47], replicated, may hold values from -0.0024414062 to 0.0024414062
- second_bias: float32 [4, 256], replicated, as said below
- second_norm: float32 [3, 2, 256], replicated, as said below
- second_head: float32 [47], replicated, as said below
Outputs:
- loss: float32 [], replicated
- new_w_in: float32 [100, 256], P(None, 'batch')
- new_w_conv: float32 [3, 512, 256], P(None, 'batch')
- new_w_head: float32 [256, 47], P('batch')
- new_mom_in: float32 [100, 256], P(None, 'batch')
- new_mom_conv: float32 [3, 512, 256], P(None, 'batch')
- new_mom_head: float32 [256, 47], P('batch')
- new_biases: float32 [4, 256], replicated
- new_norm_params: float32 [3, 2, 256], replicated
- new_head_bias: float32 [47], replicated
- new_first_bias: float32 [4, 256], replicated
- new_first_norm: float32 [3, 2, 256], replicated
- new_first_head: float32 [47], replicated
- new_second_bias: float32 [4, 256], replicated
- new_second_norm: float32 [3, 2, 256], replicated
- new_second_head: float32 [47], replicated
Inputs may be any that keep to these rules, and one draw needn't show every extreme that they name: edge_rows[b,r,0] are rows of block r; edge_rows[b,r,1] index the extended block and lie between 512 - halo_counts[b,r,0] and 2560 + halo_counts[b,r,1] - 1. `second_bias`: positive. `second_norm`: positive. `second_head`: positive.
All inputs are finite; a program needn't handle non-finite values.
Results may differ from a plain program's by a relative error of at most 0.002.
Values sent between devices are 32-bit elements; how exact they have to be, the bound alone decides.
A program may use at most 128 MiB of HBM per device.

v0:
```python
import functools
import math

import jax
import jax.numpy as jnp
from jax import lax
from jax.experimental import pallas as pl
from jax.experimental.pallas import tpu as pltpu
from jax.sharding import PartitionSpec as P

NS_STEPS = 5

f32 = jnp.float32
bf16 = jnp.bfloat16
LANES = 128
TILE = 256
highest = lax.Precision.HIGHEST
norm_epsilon = 1e-05
pair_weight = 0.05
newton_a = 3.4445
newton_b = -4.775
newton_c = 2.0315
muon_decay = 0.9
muon_rate = 0.5
muon_shrink = 0.01
adam_first_decay = 0.9
adam_second_decay = 0.999
adam_epsilon = 1e-08
adam_rate = 0.1
adam_shrink = 0.01


def swap(b, r):
    return 2 * (b // 2) + r % 2, 2 * (r // 2) + b % 2


def flat_pairs(n_batch, n_rows, move):
    pairs = []
    for b in range(n_batch):
        for r in range(n_rows):
            to = move(b, r)
            if to is not None:
                pairs.append((b * n_rows + r, to[0] * n_rows + to[1]))
    return pairs


def redeal(array, n_batch, n_rows):
    return lax.ppermute(array, ("batch", "rows"), flat_pairs(n_batch, n_rows, swap))


def peer_place(batch, block):
    two = jnp.int32(2)
    return (
        two * lax.div(batch, two) + lax.rem(block, two),
        two * lax.div(block, two) + lax.rem(batch, two),
    )


def my_place():
    return peer_place(lax.axis_index("batch"), lax.axis_index("rows"))


def order_kernel(wide, to_ref, from_ref, w_ref, key_out, w_out, col_out, lo_out, hi_out):
    to, frm = to_ref[...].astype(jnp.int32), from_ref[...].astype(jnp.int32)
    key = (((to >> 8) * wide + (frm >> 8)) << 16) | ((to & 255) << 8) | (frm & 255)
    shape3 = (16, 8, LANES)
    key = key.astype(f32).reshape(shape3)
    w = w_ref[...].reshape(shape3)
    sub = lax.broadcasted_iota(jnp.int32, shape3, 1)
    lane = lax.broadcasted_iota(jnp.int32, shape3, 2)
    vreg = lax.broadcasted_iota(jnp.int32, shape3, 0)
    place = vreg + 16 * sub + 128 * lane
    for phase in range(14):
        for bit in range(phase, -1, -1):
            down = ((place >> (phase + 1)) & 1) == 1
            if bit < 4:
                view = (16 >> (bit + 1), 2, 1 << bit, 8, LANES)
                kv, wv = key.reshape(view), w.reshape(view)
                dv = down.astype(jnp.int32).reshape(view)[:, 0] == 1
                a, b, wa, wb = kv[:, 0], kv[:, 1], wv[:, 0], wv[:, 1]
                turn = jnp.logical_xor(a > b, dv)
                key = jnp.stack([jnp.where(turn, b, a), jnp.where(turn, a, b)], 1).reshape(shape3)
                w = jnp.stack([jnp.where(turn, wb, wa), jnp.where(turn, wa, wb)], 1).reshape(shape3)
            else:
                if bit < 7:
                    axis, gap, size, pos = 1, 1 << (bit - 4), 8, sub
                else:
                    axis, gap, size, pos = 2, 1 << (bit - 7), LANES, lane
                low = (pos & gap) == 0
                kp = jnp.where(low, pltpu.roll(key, size - gap, axis), pltpu.roll(key, gap, axis))
                wp = jnp.where(low, pltpu.roll(w, size - gap, axis), pltpu.roll(w, gap, axis))
                smaller = jnp.logical_xor(low, down)
                take = jnp.where(smaller, kp, key) < jnp.where(smaller, key, kp)
                key = jnp.where(take, kp, key)
                w = jnp.where(take, wp, w)
    flat = key.reshape(LANES, LANES)
    key_out[...] = flat.T.astype(jnp.int32)
    w_out[...] = w.reshape(LANES, LANES).T
    start = (lax.broadcasted_iota(jnp.int32, (8, LANES), 1).astype(f32) * 65536.0)[None]
    below = jnp.zeros(shape3, f32)
    upto = jnp.zeros(shape3, f32)
    for c in range(LANES):
        wide_key = jnp.broadcast_to(flat[:, c : c + 1], (LANES, LANES))
        col_out[c] = (wide_key - jnp.floor(wide_key * (1.0 / 256.0)) * 256.0).astype(bf16)
        wide_key = wide_key.reshape(shape3)
        below = below + jnp.where(wide_key < start, 1.0, 0.0)
        upto = upto + jnp.where(wide_key < start + 65536.0, 1.0, 0.0)
    n_below = jnp.sum(below.reshape(LANES, LANES), axis=0, keepdims=True)
    n_upto = jnp.sum(upto.reshape(LANES, LANES), axis=0, keepdims=True)
    first = jnp.floor(n_below * (1.0 / 128.0))
    end = jnp.floor((n_upto + 127.0) * (1.0 / 128.0))
    lo_out[...] = first.astype(jnp.int32)
    hi_out[...] = jnp.where(n_upto > n_below, end, first).astype(jnp.int32)


def order_edges(to, frm, w, wide):
    vmem = pl.BlockSpec(memory_space=pltpu.VMEM)
    return pl.pallas_call(
        functools.partial(order_kernel, wide),
        out_shape=(
            jax.ShapeDtypeStruct((LANES, LANES), jnp.int32),
            jax.ShapeDtypeStruct((LANES, LANES), f32),
            jax.ShapeDtypeStruct((LANES, LANES, LANES), bf16),
            jax.ShapeDtypeStruct((1, LANES), jnp.int32),
            jax.ShapeDtypeStruct((1, LANES), jnp.int32),
        ),
        in_specs=[vmem] * 3,
        out_specs=(vmem,) * 5,
        compiler_params=pltpu.CompilerParams(vmem_limit_bytes=40 << 20),
        name="order_edges",
    )(to, frm, w)


def fill_kernel(wide, rim, chunk, parts, lo, hi, rims, key_ref, w_ref, col_ref, *refs):
    outs, sums, acc, rowacc = refs[:parts], refs[parts], refs[parts + 1], refs[parts + 2]
    i = pl.program_id(0)
    pack = 16
    shape = (TILE // pack, pack, LANES)
    rows = lax.broadcasted_iota(jnp.int32, shape, 0) * pack + lax.broadcasted_iota(jnp.int32, shape, 1)
    rows = rows.astype(f32).astype(bf16)
    lanes = lax.broadcasted_iota(jnp.int32, (LANES, LANES), 1).astype(f32)
    lanes0, lanes1 = lanes.astype(bf16), (lanes + 128.0).astype(bf16)
    one, zero = jnp.ones((), bf16), jnp.zeros((), bf16)

    def spread(row):
        return jnp.broadcast_to(row, (pack, LANES)).astype(bf16)[None]

    rowacc[...] = jnp.zeros_like(rowacc)

    def tile(j, _):
        b = i * wide + j
        first, end = lo[0, b], hi[0, b]
        end = jnp.where(jnp.logical_and(j < rim, rims[0] == 0), first, end)
        end = jnp.where(jnp.logical_and(j >= wide - rim, rims[1] == 0), first, end)
        slot = jnp.where(j < rim, wide - 2 * rim + j, jnp.where(j < wide - rim, j - rim, j))
        cols = pl.ds(pl.multiple_of(slot * TILE, TILE), TILE)

        @pl.when(end <= first)
        def _():
            for out in outs:
                out[:, cols] = jnp.zeros((TILE, TILE), bf16)

        @pl.when(end > first)
        def _():
            def part(base, c):
                row = jnp.minimum(base + c, LANES - 1)
                here = key_ref[pl.ds(row, 1), :] - (b << 16)
                if c:
                    here = jnp.where(base + c < end, here, -1)
                at = rows == spread((here >> 8).astype(f32))
                rest = w_ref[pl.ds(row, 1), :]
                left = []
                for q in range(parts):
                    piece = rest.astype(bf16).astype(f32)
                    rest = rest - piece
                    left.append(jnp.where(at, spread(piece), zero).reshape(TILE, LANES))
                col = col_ref[row]
                right = jnp.concatenate(
                    [jnp.where(col == lanes0, one, zero), jnp.where(col == lanes1, one, zero)], 1
                )
                return left, right

            def get(base):
                made = [part(base, c) for c in range(chunk)]
                lhs = jnp.concatenate([m[0][q] for q in range(parts) for m in made], 1)
                rhs = jnp.concatenate([m[1] for m in made] * parts, 0)
                return jnp.dot(lhs, rhs, preferred_element_type=f32)

            acc[...] = get(first)

            def more(t, _):
                acc[...] += get(first + t * chunk)
                return 0

            lax.fori_loop(1, lax.div(end - first + chunk - 1, chunk), more, 0)
            rest = acc[...]
            rowacc[...] += rest[:, :LANES] + rest[:, LANES:]
            for out in outs:
                piece = rest.astype(bf16)
                out[:, cols] = piece
                rest = rest - piece.astype(f32)

        return 0

    lax.fori_loop(0, wide, tile, 0)
    total = jnp.sum(rowacc[...], axis=1, keepdims=True)
    for half in range(TILE // LANES):
        column = jnp.broadcast_to(total[half * LANES : (half + 1) * LANES], (LANES, LANES))
        sums[0, half : half + 1] = column.T[0:1]


def fill(order, rims, tiles, wide, rim, parts, chunk=4):
    key, w, col, lo, hi = order
    cols = wide * TILE
    return pl.pallas_call(
        functools.partial(fill_kernel, wide, rim, chunk, parts),
        out_shape=tuple(jax.ShapeDtypeStruct((tiles * TILE, cols), bf16) for _ in range(parts))
        + (jax.ShapeDtypeStruct((tiles, TILE // LANES, LANES), f32),),
        grid_spec=pltpu.PrefetchScalarGridSpec(
            num_scalar_prefetch=3,
            grid=(tiles,),
            in_specs=[pl.BlockSpec((LANES, LANES), lambda i, *_: (0, 0))] * 2
            + [pl.BlockSpec((LANES, LANES, LANES), lambda i, *_: (0, 0, 0))],
            out_specs=tuple(pl.BlockSpec((TILE, cols), lambda i, *_: (i, 0)) for _ in range(parts))
            + (pl.BlockSpec((1, TILE // LANES, LANES), lambda i, *_: (i, 0, 0)),),
            scratch_shapes=[pltpu.VMEM((TILE, TILE), f32), pltpu.VMEM((TILE, LANES), f32)],
        ),
        compiler_params=pltpu.CompilerParams(vmem_limit_bytes=50 << 20),
        name="fill_tiles",
    )(lo, hi, rims, key, w, col)


def parts_of(x, count):
    found = []
    for q in range(count):
        piece = x.astype(bf16)
        found.append(piece)
        if q + 1 < count:
            x = x - piece.astype(f32)
    return found


def pair_list(count):
    return [(p, q) for p in range(count) for q in range(count) if p + q < count]


def dots(left, right, dims=((1,), (0,))):
    total = None
    for p, q in pair_list(len(left)):
        piece = lax.dot_general(left[p], right[q], (dims, ((), ())), preferred_element_type=f32)
        total = piece if total is None else total + piece
    return total


def remote(src, dst, send, recv, to):
    return pltpu.make_async_remote_copy(
        src_ref=src,
        dst_ref=dst,
        send_sem=send,
        recv_sem=recv,
        device_id=to,
        device_id_type=pl.DeviceIdType.MESH,
    )


def column_sums(x):
    return jnp.sum(x, axis=0, keepdims=True)


def folded(x):
    return jnp.sum(x.reshape(x.shape[0] // 8, 8, x.shape[1]), axis=0)


def plane_split(nb, n):
    cores = 2 if nb % 2 == 0 else 1
    across = 1
    while across * across * 4 <= n and n % (across * 2) == 0:
        across *= 2
    return cores, nb // cores, across, n // across


class Places:
    def __init__(self, n, nb):
        self.cores, ys, self.xs, self.zs = plane_split(nb, n)
        self.planes = ys * self.xs
        self.b, self.r = lax.axis_index("batch"), lax.axis_index("rows")
        self.core, y = lax.rem(self.b, self.cores), lax.div(self.b, self.cores)
        self.x, self.z = lax.rem(self.r, self.xs), lax.div(self.r, self.xs)
        self.spot = y * self.xs + self.x
        self.core_peer = (y * self.cores + lax.rem(self.core + 1, self.cores), self.r)
        self.peers = [self.plane_peer(k)[1] for k in range(1, self.planes)]
        self.peers += [self.column_peer(k)[1] for k in range(1, self.zs)]
        if self.cores == 2:
            self.peers.append(self.core_peer)

    def plane_peer(self, k):
        p = lax.rem(self.spot + k, self.planes)
        return p, (lax.div(p, self.xs) * self.cores + self.core, self.z * self.xs + lax.rem(p, self.xs))

    def column_peer(self, k):
        q = lax.rem(self.z + k, self.zs)
        return q, (self.b, q * self.xs + self.x)


TURNED = ((0,), (0,))
GATHERED = 3


def step_kernel(n, nb, layers, nodes, all_nodes, classes, rows_at, summed_rows, *refs):
    (x_ref, label_ref, sums_ref, bias_ref, norm_ref, head_bias_ref, pick_smem, pick_row, a1_hbm, a2_hbm) = refs[:10]
    own_in, own_conv, own_head, own_min, own_mconv, own_mhead = refs[10:16]
    pay, full_min, full_mconv, full_mhead = refs[16:20]
    (act, agg, a1, a2, p1, p2, g1, g2, gh, rim, out_rim, logit, sent, got, stat, held, w_in, w_conv, w_head,
     wt, a_sem, stat_send, stat_recv, rim_send, rim_recv, pair_send, pair_recv, w_send, w_recv, w_own, sum_send, sum_recv,
     ready, normed, keep) = refs[20:]
    rows, width = act.shape[1], act.shape[2]
    halo = rim.shape[2]
    a, ps, gs = (a1, a2), (p1, p2), (g1, g2)
    here_b, here_r = lax.axis_index("batch"), lax.axis_index("rows")
    batch, block = my_place()
    first, last = block == 0, block == n - 1
    not_first, not_last = jnp.logical_not(first), jnp.logical_not(last)

    barrier = pltpu.get_barrier_semaphore()
    for k in range(1, n):
        pl.semaphore_signal(
            barrier, inc=1, device_id=peer_place(batch, lax.rem(block + k, n)), device_id_type=pl.DeviceIdType.MESH
        )
    for k in range(1, nb):
        pl.semaphore_signal(
            barrier, inc=1, device_id=(lax.rem(here_b + k, nb), here_r), device_id_type=pl.DeviceIdType.MESH
        )
    places = Places(n, nb)
    for peer in places.peers:
        pl.semaphore_signal(barrier, inc=1, device_id=peer, device_id_type=pl.DeviceIdType.MESH)
    height = 512
    for s in range(rows // height):
        span = pl.ds(s * height, height)
        for q, (src, dst) in enumerate(zip((a1_hbm, a2_hbm), a)):
            pltpu.make_async_copy(src.at[span], dst.at[span], a_sem.at[2 * s + q]).start()
    pl.semaphore_wait(barrier, n - 1 + nb - 1 + len(places.peers))

    def gathers(item, src, dst):
        span = src.shape[-2]
        lead = (slice(None),) * (len(src.shape) - 2)
        mine = dst.at[lead + (pl.ds(pl.multiple_of(here_b * span, 8), span),)]
        copies = [pltpu.make_async_copy(src, mine, w_own.at[item])]
        for k in range(1, nb):
            copies.append(remote(src, mine, w_send.at[item, k], w_recv.at[item, k], (lax.rem(here_b + k, nb), here_r)))
        return copies

    def gather(item, src, dst):
        copies = gathers(item, src, dst)
        for copy in copies:
            copy.start()
        return copies

    def arrived(copies):
        for copy in copies:
            copy.wait()

    in_copies = gather(0, own_in, w_in)
    for q in range(layers):
        gather(2 + q, own_conv.at[q], w_conv.at[q])
    head_copies = gather(1, own_head, w_head)

    def stat_copies(e):
        return [
            remote(stat.at[e], held.at[e, k], stat_send.at[e, k], stat_recv.at[e, k], peer_place(batch, lax.rem(block + k, n)))
            for k in range(1, n)
        ]

    def stats_start(e):
        held[e, 0] = stat[e]
        for copy in stat_copies(e):
            copy.start()

    def stats_finish(e):
        arrived(stat_copies(e))
        total = held[e, lax.rem(block, n)]
        for q in range(1, n):
            total = total + held[e, lax.rem(block + n - q, n)]
        return total

    def rims_of(e, low_src, high_src):
        slot = lax.rem(e, 2)
        return (
            remote(low_src, rim.at[slot, 1], rim_send.at[e, 1], rim_recv.at[e, 1], peer_place(batch, lax.rem(block + n - 1, n))),
            remote(high_src, rim.at[slot, 0], rim_send.at[e, 0], rim_recv.at[e, 0], peer_place(batch, lax.rem(block + 1, n))),
        )

    def start_if(condition, copy):
        @pl.when(condition)
        def _():
            copy.start()

    def rims_sent(copies):
        @pl.when(not_first)
        def _():
            copies[0].wait_send()

        @pl.when(not_last)
        def _():
            copies[1].wait_send()

    tile = 256
    tiles = rows // tile

    def rows_of(s, size):
        return pl.ds(pl.multiple_of(s * size, size), size)

    zeros8 = jnp.zeros((8, width), f32)

    arrived(in_copies)
    turned_in = parts_of(w_in[...].T, 3)

    def project(s, _):
        span = rows_of(s, tile)
        act[0, span] = dots(parts_of(x_ref[span, :], 3), turned_in) + bias_ref[0]
        return 0

    lax.fori_loop(0, tiles, project, 0)
    stat[0] = jnp.zeros((2, width), f32)
    own_cols, rim_cols = pl.ds(0, rows), pl.ds(rows, 2 * halo)

    def set_norm(l, totals):
        mean = totals[0:1] * (1.0 / nodes)
        inverse = lax.rsqrt(totals[1:2] * (1.0 / nodes) - mean * mean + norm_epsilon)
        under = lax.max(l - 1, 0)
        scale = norm_ref[under, 0:1] * inverse
        offset = norm_ref[under, 1:2] - mean * scale
        plain = l == 0
        normed[l, 0:1] = jnp.where(plain, 0.0, mean)
        normed[l, 1:2] = jnp.where(plain, 1.0, inverse)
        normed[l, 2:3] = jnp.where(plain, 1.0, scale)
        normed[l, 3:4] = jnp.where(plain, 0.0, offset)

    def forward(l, _):
        copies = rims_of(l, act.at[l, pl.ds(0, halo)], act.at[l, pl.ds(rows - halo, halo)])
        start_if(not_first, copies[0])
        start_if(not_last, copies[1])
        stats_start(l)

        def split(s, _):
            span = rows_of(s, tile)
            for dst, piece in zip(ps, parts_of(act[l, span], 2)):
                dst[span, :] = piece
            return 0

        lax.fori_loop(0, tiles, split, 0)

        def own(s, _):
            span = rows_of(s, height)

            @pl.when(l == 0)
            def _():
                for q, (src, dst) in enumerate(zip((a1_hbm, a2_hbm), a)):
                    pltpu.make_async_copy(src.at[span], dst.at[span], a_sem.at[2 * s + q]).wait()

            agg[l, span] = dots([q[span, own_cols] for q in a], [q[own_cols, :] for q in ps])
            return 0

        lax.fori_loop(0, rows // height, own, 0)
        set_norm(l, stats_finish(l))
        slot = lax.rem(l, 2)
        for which, gone in ((0, first), (1, last)):
            @pl.when(gone)
            def _():
                rim[slot, which] = jnp.zeros((halo, width), f32)

            @pl.when(jnp.logical_not(gone))
            def _():
                remote(rim.at[slot, which], rim.at[slot, which], rim_send.at[l, which], rim_recv.at[l, which],
                       peer_place(batch, lax.rem(block + 1, n))).wait_recv()

            for dst, piece in zip(ps, parts_of(rim[slot, which], 2)):
                dst[pl.ds(rows + which * halo, halo), :] = piece

        def rims_in(s, _):
            span = rows_of(s, height)
            agg[l, span] += dots([q[span, rim_cols] for q in a], [q[rim_cols, :] for q in ps])
            return 0

        lax.fori_loop(0, rows // height, rims_in, 0)
        arrived(gathers(2 + l, own_conv.at[l], w_conv.at[l]))
        weights = parts_of(w_conv[l], 3)
        bias = bias_ref[l + 1]
        scale, offset = normed[l, 2:3], normed[l, 3:4]

        def finish(s, sums):
            span = rows_of(s, tile)
            row_sum = jnp.concatenate(
                [jnp.broadcast_to(sums_ref[s, i : i + 1], (LANES, LANES)).T for i in range(tile // LANES)], 0
            )
            found = agg[l, span] * scale + jnp.concatenate([row_sum] * (width // LANES), 1) * offset
            agg[l, span] = found
            h = act[l, span] * scale + offset
            pre = dots(parts_of(jnp.concatenate([h, found], 1), 3), weights) + bias
            active = jnp.maximum(pre, 0.0)
            act[l + 1, span] = active
            return sums[0] + folded(active), sums[1] + folded(active * active)

        sums = lax.fori_loop(0, tiles, finish, (zeros8, zeros8))
        stat[l + 1, 0:1] = column_sums(sums[0])
        stat[l + 1, 1:2] = column_sums(sums[1])
        rims_sent(copies)
        return 0

    lax.fori_loop(0, layers, forward, 0)

    stats_start(layers)
    base = 2 + layers
    late = [gather(base, own_min, full_min), gather(base + 1, own_mhead, full_mhead), gather(base + 2, own_mconv, full_mconv)]
    arrived(head_copies)
    head_parts = parts_of(w_head[...], 3)
    head_turned = parts_of(w_head[...].T, 2)
    set_norm(layers, stats_finish(layers))
    top_scale, top_offset = normed[layers, 2:3], normed[layers, 3:4]
    top_mean, top_inverse = normed[layers, 0:1], normed[layers, 1:2]

    def top(span):
        return act[layers, span] * top_scale + top_offset

    def classify(s, _):
        span = rows_of(s, tile)
        logit[span, :] = dots(parts_of(top(span), 3), head_parts) + head_bias_ref[...]
        return 0

    lax.fori_loop(0, tiles, classify, 0)
    per = pick_smem.shape[0] // n
    sent[...] = jnp.zeros_like(sent)
    for d in range(n):
        for k in range(per):
            sent[d, k : k + 1] = logit[pl.ds(pick_smem[d * per + k], 1), :]
    pair_copies = []
    for k in range(1, n):
        peer = lax.rem(block + k, n)
        copy = remote(sent.at[peer], got.at[k], pair_send.at[k], pair_recv.at[k], peer_place(batch, peer))
        copy.start()
        pair_copies.append(copy)
    got[0] = sent[block]
    lane = lax.broadcasted_iota(jnp.int32, (tile, LANES), 1)
    real = lane < classes

    def soften(s, loss):
        span = rows_of(s, tile)
        z = logit[span, :]
        top_z = jnp.max(jnp.where(real, z, -jnp.inf), axis=1, keepdims=True)
        e = jnp.where(real, jnp.exp(z - top_z), 0.0)
        total = jnp.sum(e, axis=1, keepdims=True)
        named = [
            jnp.broadcast_to(label_ref[pl.ds(s * (tile // LANES) + i, 1), :], (LANES, LANES)).T for i in range(tile // LANES)
        ]
        hot = jnp.logical_and(real, lane.astype(f32) == jnp.concatenate(named, 0))
        logit[span, :] = e / total - jnp.where(hot, 1.0, 0.0)
        part = jnp.where(lane == 0, top_z + jnp.log(total), 0.0) - jnp.where(hot, z, 0.0)
        return loss + folded(part)

    loss = lax.fori_loop(0, tiles, soften, jnp.zeros((8, LANES), f32))
    arrived(pair_copies)
    gaps = []
    for d in range(n):
        gaps.append(sent[d] - got[lax.rem(block + n - d, n)])
    gap = jnp.concatenate(gaps, 0)
    loss = loss + pair_weight * folded(gap * gap)
    spare = pick_row.shape[1] - gap.shape[0]
    if spare:
        gap = jnp.concatenate([gap, jnp.zeros((spare, LANES), f32)], 0)
    gap_parts = parts_of(gap * (4.0 * pair_weight), 3)
    at_head, at_small = rows_at[1], rows_at[2]
    small = layers + 1

    def finish_head(s, sums):
        span = rows_of(s, tile)
        spot = lax.broadcasted_iota(jnp.int32, (tile, pick_row.shape[1]), 0) + s * tile
        chosen = jnp.where(spot == pick_row[...], 1.0, 0.0).astype(bf16)
        add = None
        for piece in gap_parts:
            v = jnp.dot(chosen, piece, preferred_element_type=f32)
            add = v if add is None else add + v
        grad = (logit[span, :] + add) * (1.0 / all_nodes)
        grad_parts = parts_of(grad, 2)
        h = top(span)
        back = dots(grad_parts, head_turned)
        gh[span, :] = back
        ready_top = (act[layers, span] - top_mean) * top_inverse
        return (
            sums[0] + dots(parts_of(h, 2), grad_parts, TURNED),
            sums[1] + folded(grad),
            sums[2] + folded(back),
            sums[3] + folded(back * ready_top),
        )

    begin = (
        jnp.zeros((width, LANES), f32),
        jnp.zeros((8, LANES), f32),
        jnp.zeros((8, width), f32),
        jnp.zeros((8, width), f32),
    )
    sums = lax.fori_loop(0, tiles, finish_head, begin)
    half = width // 2
    pay[pl.ds(at_head, half), :] = jnp.concatenate([sums[0][:half], sums[0][half:]], 1)
    tail = pl.ds(at_small, summed_rows - at_small)
    pay[tail, :] = jnp.zeros((summed_rows - at_small, width), f32)
    at_norm = at_small + small
    at_last = at_norm + 2 * layers
    pay[at_last : at_last + 1, 0:LANES] = column_sums(sums[1])
    pay[at_last + 1 : at_last + 2, 0:LANES] = column_sums(loss)
    after = layers + 1
    stat[after, 0:1] = column_sums(sums[2])
    stat[after, 1:2] = column_sums(sums[3])
    stats_start(after)

    big = 2 * width

    def conv_rows(l):
        return pl.multiple_of(jnp.where(l == 0, 0, summed_rows + (l - 1) * big), 8)

    def told(which):
        for peer in places.peers:
            pl.semaphore_signal(ready.at[which], inc=1, device_id=peer, device_id_type=pl.DeviceIdType.MESH)

    cores, planes, zs = places.cores, places.planes, places.zs
    core, spot = places.core, places.spot
    piece_rows = big // cores
    block_rows = piece_rows // planes

    def part(ref, index, count):
        return ref.at[pl.ds(pl.multiple_of(index * count, 8), count)]

    class Sum:
        def __init__(self, l):
            self.which, room = l - 1, act.at[l + 1]
            self.local = pay.at[pl.ds(conv_rows(l), big)]
            self.whole = room.at[pl.ds(0, big)]
            spots = [piece_rows, piece_rows, piece_rows, block_rows, block_rows * zs]
            views, at = [], big
            for count in spots:
                views.append(room.at[pl.ds(at, count)])
                at += count
            self.got1, self.sum1, self.got2, self.sum2, self.got3 = views

        def copies(self, stage):
            found = []

            def add(i, src, dst, to):
                found.append(remote(src, dst, sum_send.at[self.which, i], sum_recv.at[self.which, i], to))

            if stage == 0 and cores == 2:
                add(0, part(self.local, 1 - core, piece_rows), self.got1, places.core_peer)
            if stage == 1:
                for k in range(1, planes):
                    p, to = places.plane_peer(k)
                    add(k, part(self.sum1, p, block_rows), part(self.got2, k, block_rows), to)
            if stage == 2:
                for k in range(1, zs):
                    add(planes + k, self.sum2, part(self.got3, k, block_rows), places.column_peer(k)[1])
            if stage == 3:
                mine = part(self.whole, core * planes + spot, block_rows)
                for k in range(1, planes):
                    add(planes + zs + k, mine, mine, places.plane_peer(k)[1])
            if stage == 4 and cores == 2:
                mine = part(self.whole, core, piece_rows)
                add(2 * planes + zs, mine, mine, places.core_peer)
            return found

        def go(self, stage):
            if stage == 0:
                pl.semaphore_wait(ready.at[self.which], len(places.peers))
            else:
                arrived(self.copies(stage - 1))
            if stage == 1:
                total = part(self.local, core, piece_rows)[...]
                if cores == 2:
                    total = total + self.got1[...]
                self.sum1[...] = total
            if stage == 2:
                total = part(self.sum1, spot, block_rows)[...]
                for k in range(1, planes):
                    total = total + part(self.got2, k, block_rows)[...]
                self.sum2[...] = total
                self.got3[pl.ds(0, block_rows), :] = total
            if stage == 3:
                total = part(self.got3, lax.rem(places.z, zs), block_rows)[...]
                for q in range(1, zs):
                    total = total + part(self.got3, lax.rem(places.z + zs - q, zs), block_rows)[...]
                part(self.whole, core * planes + spot, block_rows)[...] = total
            if stage == 5:
                self.local[...] = self.whole[...]
            for copy in self.copies(stage):
                copy.start()

    def backward(turn, _):
        l = layers - 1 - turn
        e = after + turn

        def advance(stage):
            @pl.when(turn > 0)
            def _():
                Sum(l + 1).go(stage)

        keep[l, 0:1] = stat[e, 1:2]
        keep[l, 1:2] = stat[e, 0:1]
        for q, piece in enumerate(parts_of(w_conv[l].T, 2)):
            wt[q] = piece
        gain = norm_ref[l, 0:1]
        totals = stats_finish(e) * gain * (1.0 / nodes)
        mean, inverse = normed[l + 1, 0:1], normed[l + 1, 1:2]

        def enter(s, total):
            span = rows_of(s, tile)
            active = act[l + 1, span]
            rated = (active - mean) * inverse
            grad = inverse * (gh[span, :] * gain - totals[0:1] - rated * totals[1:2])
            grad = jnp.where(active > 0.0, grad, 0.0)
            pieces = parts_of(grad, 2)
            for dst, piece in zip(gs, pieces):
                dst[span, :] = piece
            joined = dots(pieces, [wt[0], wt[1]])
            gh[span, :] = joined[:, :width]
            for dst, piece in zip(ps, parts_of(joined[:, width:], 2)):
                dst[span, :] = piece
            return total + folded(grad)

        total = lax.fori_loop(0, tiles, enter, zeros8)
        keep[l, 2:3] = column_sums(total)

        @pl.when(l > 0)
        def _():
            told(l - 1)

        advance(1)
        copies = rims_of(e, out_rim.at[0], out_rim.at[1])

        def rims_out(which, _):
            cols = pl.ds(pl.multiple_of(rows + which * halo, 128), halo)
            out_rim[which] = dots([q[:, cols] for q in a], [q[own_cols, :] for q in ps], TURNED)
            for at, go in ((0, not_first), (1, not_last)):
                start_if(jnp.logical_and(go, which == at), copies[at])
            return 0

        lax.fori_loop(0, 2, rims_out, 0)
        advance(2)

        def spread_back(s, _):
            span = rows_of(s, height)
            gh[span, :] += dots([q[:, span] for q in a], [q[own_cols, :] for q in ps], TURNED)
            return 0

        lax.fori_loop(0, rows // height, spread_back, 0)
        advance(3)
        slot = lax.rem(e, 2)
        for which, go, start in ((1, not_last, rows - halo), (0, not_first, 0)):
            @pl.when(go)
            def _():
                remote(rim.at[slot, which], rim.at[slot, which], rim_send.at[e, which], rim_recv.at[e, which],
                       peer_place(batch, lax.rem(block + 1, n))).wait_recv()
                gh[pl.ds(start, halo), :] += rim[slot, which]

        below_mean, below_inverse = normed[l, 0:1], normed[l, 1:2]

        def tail_sums(s, sums):
            span = rows_of(s, tile)
            grad = gh[span, :]
            return sums[0] + folded(grad), sums[1] + folded(grad * ((act[l, span] - below_mean) * below_inverse))

        sums = lax.fori_loop(0, tiles, tail_sums, (zeros8, zeros8))
        stat[e + 1, 0:1] = column_sums(sums[0])
        stat[e + 1, 1:2] = column_sums(sums[1])

        @pl.when(l > 0)
        def _():
            stats_start(e + 1)

        rims_sent(copies)
        advance(4)
        base = conv_rows(l)
        where = pl.ds(base, width)
        under = pl.ds(pl.multiple_of(base + width, 8), width)
        scale, offset = normed[l, 2:3], normed[l, 3:4]
        pay[pl.ds(base, big), :] = jnp.zeros((big, width), f32)

        def weigh(s, _):
            span = rows_of(s, height)
            h = act[l, span] * scale + offset
            grad = [q[span, :] for q in gs]
            pay[where, :] += dots(parts_of(h, 2), grad, TURNED)
            pay[under, :] += dots(parts_of(agg[l, span], 2), grad, TURNED)
            return 0

        lax.fori_loop(0, rows // height, weigh, 0)
        advance(5)

        @pl.when(l > 0)
        def _():
            Sum(l).go(0)

        return 0

    lax.fori_loop(0, layers, backward, 0)
    pay[at_small : at_small + 1, :] = stat[after + layers, 0:1]
    for l in range(layers):
        pay[at_norm + 2 * l : at_norm + 2 * l + 2, :] = keep[l, 0:2]
        pay[at_small + 1 + l : at_small + 2 + l, :] = keep[l, 2:3]
    feat = x_ref.shape[1]
    pay[pl.ds(rows_at[0], rows_at[1] - rows_at[0]), :] = jnp.zeros((rows_at[1] - rows_at[0], width), f32)

    def weigh_in(s, total):
        span = rows_of(s, height)
        return total + dots(parts_of(x_ref[span, :], 2), parts_of(gh[span, :], 2), TURNED)

    pay[pl.ds(rows_at[0], feat), :] = lax.fori_loop(0, rows // height, weigh_in, jnp.zeros((feat, width), f32))
    for copies in late:
        arrived(copies)


def step_call(n, nb, layers, nodes, all_nodes, classes, rows_at, summed_rows, x, labels, sums, biases, norms, head_bias,
              picks, pick_row, adjacency, shards):
    rows = x.shape[0]
    width = biases.shape[1]
    cols = adjacency[0].shape[1]
    halo = (cols - rows) // 2
    feat = x.shape[1]
    vmem = pl.BlockSpec(memory_space=pltpu.VMEM)
    smem = pl.BlockSpec(memory_space=pltpu.SMEM)
    hbm = pl.BlockSpec(memory_space=pl.ANY)
    dma = pltpu.SemaphoreType.DMA
    items = 2 + layers + 3
    exchanges = 2 * layers + 1
    _, ys, across, zs = plane_split(nb, n)
    hops = 2 * ys * across + zs + 1
    return pl.pallas_call(
        functools.partial(step_kernel, n, nb, layers, nodes, all_nodes, classes, rows_at, summed_rows),
        out_shape=(
            jax.ShapeDtypeStruct((summed_rows + (layers - 1) * 2 * width, width), f32),
            jax.ShapeDtypeStruct((width, feat), f32),
            jax.ShapeDtypeStruct((layers, 2 * width, width), f32),
            jax.ShapeDtypeStruct((width, LANES), f32),
        ),
        in_specs=[vmem] * 6 + [smem, vmem] + [hbm] * 8,
        out_specs=(vmem, hbm, hbm, hbm),
        scratch_shapes=[
            pltpu.VMEM((layers + 1, rows, width), f32),
            pltpu.VMEM((layers, rows, width), f32),
            pltpu.VMEM((rows, cols), bf16),
            pltpu.VMEM((rows, cols), bf16),
            pltpu.VMEM((cols, width), bf16),
            pltpu.VMEM((cols, width), bf16),
            pltpu.VMEM((rows, width), bf16),
            pltpu.VMEM((rows, width), bf16),
            pltpu.VMEM((rows, width), f32),
            pltpu.VMEM((2, 2, halo, width), f32),
            pltpu.VMEM((2, halo, width), f32),
            pltpu.VMEM((rows, LANES), f32),
            pltpu.VMEM((n, 8, LANES), f32),
            pltpu.VMEM((n, 8, LANES), f32),
            pltpu.VMEM((exchanges + 1, 2, width), f32),
            pltpu.VMEM((exchanges, n, 2, width), f32),
            pltpu.VMEM((width, feat), f32),
            pltpu.VMEM((layers, 2 * width, width), f32),
            pltpu.VMEM((width, LANES), f32),
            pltpu.VMEM((2, width, 2 * width), bf16),
            dma((2 * rows // 512,)),
            dma((exchanges, n)),
            dma((exchanges, n)),
            dma((exchanges, 2)),
            dma((exchanges, 2)),
            dma((n,)),
            dma((n,)),
            dma((items, nb)),
            dma((items, nb)),
            dma((items,)),
            dma((layers - 1, hops)),
            dma((layers - 1, hops)),
            pltpu.SemaphoreType.REGULAR((layers - 1,)),
            pltpu.VMEM((layers + 1, 4, width), f32),
            pltpu.VMEM((layers, 4, width), f32),
        ],
        compiler_params=pltpu.CompilerParams(collective_id=1, has_side_effects=True, vmem_limit_bytes=63 << 20),
        name="forward_backward",
    )(x, labels, sums, biases[:, None], norms, head_bias, picks, pick_row, *adjacency, *shards)


def update_kernel(n, nb, layers, all_nodes, rows_at, classes, ns_parts, scales, summed_rows, pay, mom_in, mom_conv, mom_head, w_in,
                  w_conv, w_head, biases, norms, head_bias, fb, fn, fh, sb, sn, sh, power, *refs):
    (loss_o, in_o, conv_o, head_o, min_o, mconv_o, mhead_o, b_o, n_o, h_o, fb_o, fn_o, fh_o, sb_o, sn_o, sh_o) = refs[:16]
    (got1, sum1, got2, sum2, got3, full, gram, poly, small_gram, small_poly, mconv, send, recv) = refs[16:]
    places = Places(n, nb)
    cores, planes, zs = places.cores, places.planes, places.zs
    core, spot, z = places.core, places.spot, places.z
    plane_peer, column_peer, core_peer = places.plane_peer, places.column_peer, places.core_peer
    here_b = places.b
    width = w_conv.shape[2]
    barrier = pltpu.get_barrier_semaphore()
    for peer in places.peers:
        pl.semaphore_signal(barrier, inc=1, device_id=peer, device_id_type=pl.DeviceIdType.MESH)

    def kdot(left, right, dims=((1,), (0,))):
        return dots(parts_of(left, ns_parts), parts_of(right, ns_parts), dims)

    def eye(k):
        return (lax.broadcasted_iota(jnp.int32, (k, k), 0) == lax.broadcasted_iota(jnp.int32, (k, k), 1)).astype(f32)

    def begin(moment, grams, i):
        size = jnp.sqrt(jnp.sum(moment * moment)) + 1e-07
        g = kdot(moment, moment, TURNED) / (size * size)
        grams[i] = g
        return size

    def step(grams, polys, which, early, late):
        k = grams.shape[1]
        count = len(which)
        a1 = [grams[i] for i in which]
        a2 = [kdot(v, v) for v in a1]
        p = [newton_a * eye(k) + newton_b * v + newton_c * u for v, u in zip(a1, a2)]
        if early:
            q = p
        else:
            q = [kdot(v, polys[i]) for i, v in zip(which, p)]
        if not late:
            pa = [kdot(v, u) for v, u in zip(p, a1)]
            nxt = [kdot(v, u) for v, u in zip(pa, p)]
        for j in range(count):
            polys[which[j]] = q[j]
            if not late:
                grams[which[j]] = nxt[j]

    sizes = {}
    ready = tuple(range(1, layers))

    def start_ready():
        for l in ready:
            mconv[l] = muon_decay * mom_conv[l] + pay[summed_rows + (l - 1) * 2 * width : summed_rows + l * 2 * width]
            sizes[l] = begin(mconv[l], gram, l)

    def middle(count, grams, polys, which):
        lax.fori_loop(0, count, lambda _, c: (step(grams, polys, which, False, False), c)[1], 0)

    pl.semaphore_wait(barrier, len(places.peers))
    used = [0]

    def go(src, dst, to):
        i = used[0]
        used[0] += 1
        copy = remote(src, dst, send.at[i], recv.at[i], to)
        copy.start()
        return copy

    def settle(copies):
        for copy in copies:
            copy.wait()

    half_rows = summed_rows // cores
    block_rows = half_rows // planes
    m = block_rows // zs

    def part(ref, index, count):
        return ref.at[pl.ds(pl.multiple_of(index * count, 8), count)]

    if cores == 2:
        copies = [go(part(pay, 1 - core, half_rows), got1, core_peer)]
        start_ready()
        settle(copies)
        sum1[...] = part(pay, core, half_rows)[...] + got1[...]
    else:
        start_ready()
        sum1[...] = pay[pl.ds(0, half_rows), :]
    copies = []
    for k in range(1, planes):
        p, to = plane_peer(k)
        copies.append(go(part(sum1, p, block_rows), got2.at[k], to))
    step(gram, poly, ready, True, False)
    middle(1, gram, poly, ready)
    settle(copies)
    total = part(sum1, spot, block_rows)[...]
    for k in range(1, planes):
        total = total + got2[k]
    sum2[...] = total
    copies = []
    for k in range(1, zs):
        q, to = column_peer(k)
        copies.append(go(part(sum2, q, m), got3.at[k], to))
    middle(1, gram, poly, ready)
    settle(copies)
    total = part(sum2, z, m)[...]
    for k in range(1, zs):
        total = total + got3[k]
    block = core * planes + spot
    mine = part(full, block * zs + z, m)
    mine[...] = total
    copies = [go(mine, mine, column_peer(k)[1]) for k in range(1, zs)]
    middle(1, gram, poly, ready)
    settle(copies)
    mine = part(full, block, block_rows)
    copies = [go(mine, mine, plane_peer(k)[1]) for k in range(1, planes)]
    step(gram, poly, ready, False, True)
    scale_in, scale_conv, scale_head = scales
    span = w_conv.shape[1]

    def turn_conv(l):
        own = mconv[l, pl.ds(pl.multiple_of(here_b * span, 8), span)]
        mconv_o[l] = own
        w = w_conv[l]
        turn = kdot(own, poly[l]) * (scale_conv / sizes[l])
        conv_o[l] = w - muon_rate * (turn + muon_shrink * w)

    for l in ready:
        turn_conv(l)
    settle(copies)
    if cores == 2:
        mine = part(full, core, half_rows)
        settle([go(mine, mine, core_peer)])
    summed = full[...]
    mconv[0] = muon_decay * mom_conv[0] + summed[: 2 * width]
    sizes[0] = begin(mconv[0], gram, 0)
    feat = w_in.shape[1]
    half = width // 2
    grad_in = summed[rows_at[0] : rows_at[0] + LANES].T
    grad_head = summed[rows_at[1] : rows_at[1] + half]
    moment_in = muon_decay * mom_in[...] + jnp.where(lax.broadcasted_iota(jnp.int32, (width, LANES), 1) < feat, grad_in, 0.0)
    moment_head = muon_decay * mom_head[...] + jnp.concatenate([grad_head[:, :LANES], grad_head[:, LANES:]], 0)
    sizes[layers] = begin(moment_in, small_gram, 0)
    sizes[layers + 1] = begin(moment_head, small_gram, 1)

    def both(early, late):
        step(gram, poly, (0,), early, late)
        step(small_gram, small_poly, (0, 1), early, late)

    both(True, False)
    lax.fori_loop(1, NS_STEPS - 1, lambda _, c: (both(False, False), c)[1], 0)
    both(False, True)
    turn_conv(0)
    span = w_in.shape[0]
    mconv[0, pl.ds(0, width), 0:LANES] = moment_in
    mconv[0, pl.ds(0, width), LANES : 2 * LANES] = moment_head
    own = mconv[0, pl.ds(pl.multiple_of(here_b * span, 8), span), 0:LANES]
    min_o[...] = own[:, :feat]
    w = w_in[...]
    turn = kdot(own, small_poly[0]) * (scale_in / sizes[layers])
    in_o[...] = w - muon_rate * (turn[:, :feat] + muon_shrink * w)
    span = w_head.shape[0]
    own = mconv[0, pl.ds(pl.multiple_of(here_b * span, 8), span), LANES : 2 * LANES]
    mhead_o[...] = own[:, :classes]
    w = w_head[...]
    turn = kdot(own, small_poly[1]) * (scale_head / sizes[layers + 1])
    head_o[...] = w - muon_rate * (turn[:, :classes] + muon_shrink * w)

    def adamw(param, grad, first, second, outs):
        first = adam_first_decay * first + (1.0 - adam_first_decay) * grad
        second = adam_second_decay * second + (1.0 - adam_second_decay) * grad * grad
        first_hat = first / power[0]
        second_hat = second / power[1]
        outs[0][...] = param - adam_rate * (first_hat / (jnp.sqrt(second_hat) + adam_epsilon) + adam_shrink * param)
        outs[1][...] = first
        outs[2][...] = second

    at = rows_at[2]
    adamw(biases[...], summed[at : at + layers + 1], fb[...], sb[...], (b_o, fb_o, sb_o))
    at = at + layers + 1
    adamw(norms[...], summed[at : at + 2 * layers], fn[...], sn[...], (n_o, fn_o, sn_o))
    at = at + 2 * layers
    adamw(head_bias[...], summed[at : at + 1, :classes], fh[...], sh[...], (h_o, fh_o, sh_o))
    loss_o[...] = jnp.sum(summed[at + 1 : at + 2], axis=1, keepdims=True) / all_nodes


def update_call(n, nb, layers, all_nodes, rows_at, classes, ns_parts, scales, summed_rows, pay, moments, shards, smalls, power):
    cores, ys, xs, zs = plane_split(nb, n)
    planes = ys * xs
    width = pay.shape[1]
    m = summed_rows // (n * nb)
    w_in, w_conv, w_head = shards
    vmem = pl.BlockSpec(memory_space=pltpu.VMEM)
    smem = pl.BlockSpec(memory_space=pltpu.SMEM)
    like = [jax.ShapeDtypeStruct(v.shape, f32) for v in (w_in, w_conv, w_head)]
    like_small = [jax.ShapeDtypeStruct(v.shape, f32) for v in smalls[:3]]
    copies = 2 * (planes + zs)
    return pl.pallas_call(
        functools.partial(update_kernel, n, nb, layers, all_nodes, rows_at, classes, ns_parts, scales, summed_rows),
        out_shape=tuple([jax.ShapeDtypeStruct((1, 1), f32)] + like + like + like_small * 3),
        in_specs=[vmem] * 16 + [smem],
        out_specs=(vmem,) * 16,
        scratch_shapes=[
            pltpu.VMEM((zs * planes * m, width), f32),
            pltpu.VMEM((zs * planes * m, width), f32),
            pltpu.VMEM((planes, zs * m, width), f32),
            pltpu.VMEM((zs * m, width), f32),
            pltpu.VMEM((zs, m, width), f32),
            pltpu.VMEM((summed_rows, width), f32),
            pltpu.VMEM((layers, width, width), f32),
            pltpu.VMEM((layers, width, width), f32),
            pltpu.VMEM((2, LANES, LANES), f32),
            pltpu.VMEM((2, LANES, LANES), f32),
            pltpu.VMEM((layers, 2 * width, width), f32),
            pltpu.SemaphoreType.DMA((copies,)),
            pltpu.SemaphoreType.DMA((copies,)),
        ],
        compiler_params=pltpu.CompilerParams(collective_id=2, has_side_effects=True, vmem_limit_bytes=48 << 20),
        name="sum_and_update",
    )(pay, *moments, *shards, *smalls, power)


NS_PARTS = 3


def per_device(
    n_batch,
    n_rows,
    features,
    edge_rows,
    edge_weight,
    halo_counts,
    labels,
    pair_rows,
    step,
    w_in,
    w_conv,
    w_head,
    biases,
    norm_params,
    head_bias,
    mom_in,
    mom_conv,
    mom_head,
    first_bias,
    first_norm,
    first_head,
    second_bias,
    second_norm,
    second_head,
):
    rows_dev = features.shape[1]
    halo_rows = rows_dev // 4
    edge_count = edge_rows.shape[3]
    layers, hid = w_conv.shape[0], w_conv.shape[2]
    feat, classes = w_in.shape[0], w_head.shape[1]
    pairs = pair_rows.shape[3]
    node_count = rows_dev * n_rows
    all_nodes = node_count * n_batch
    flat = [
        edge_rows.reshape(2 * edge_count).astype(f32),
        edge_weight.reshape(edge_count),
        labels.reshape(rows_dev).astype(f32),
        pair_rows.reshape(n_rows * pairs).astype(f32),
    ]
    flat = jnp.concatenate(flat)
    flat = jnp.pad(flat, (0, -flat.shape[0] % (8 * LANES))).reshape(-1, LANES)
    flat = redeal(flat, n_batch, n_rows)
    inputs = redeal(features, n_batch, n_rows)[0]
    e = edge_count // LANES
    block = my_place()[1]
    wide = (rows_dev + 2 * halo_rows) // TILE
    rims = jnp.stack([(block > 0).astype(jnp.int32), (block < n_rows - 1).astype(jnp.int32)])
    order = order_edges(flat[:e], flat[e : 2 * e], flat[2 * e : 3 * e], wide)
    *adjacency, row_sums = fill(order, rims, rows_dev // TILE, wide, halo_rows // TILE, 2)
    label_rows = rows_dev // LANES
    node_labels = flat[3 * e : 3 * e + label_rows]
    picks = flat[3 * e + label_rows :].reshape(-1)[: n_rows * pairs].astype(jnp.int32)
    spread = jnp.pad(picks.reshape(n_rows, pairs), ((0, 0), (0, 8 - pairs)), constant_values=-1).reshape(1, n_rows * 8)
    spread = jnp.pad(spread, ((0, 0), (0, -spread.shape[1] % LANES)), constant_values=-1)
    at_in = 2 * hid
    at_head = at_in + -(-feat // 8) * 8
    at_small = at_head + hid // 2
    used = at_small + layers + 1 + 2 * layers + 2
    unit = 8 * n_rows * n_batch
    pay_rows = -(-used // unit) * unit
    rows_at = (at_in, at_head, at_small)
    turned = [
        w_in.T,
        w_conv,
        jnp.pad(w_head, ((0, 0), (0, LANES - classes))),
        mom_in.T,
        mom_conv,
        jnp.pad(mom_head, ((0, 0), (0, LANES - classes))),
    ]
    pay, full_min, full_mconv, full_mhead = step_call(
        n_rows,
        n_batch,
        layers,
        node_count,
        all_nodes,
        classes,
        rows_at,
        pay_rows,
        inputs,
        node_labels,
        row_sums,
        biases,
        norm_params,
        jnp.pad(head_bias, (0, LANES - classes))[None],
        picks,
        spread,
        adjacency,
        turned,
    )
    count = step[0].astype(f32)
    power = jnp.stack([1.0 - jnp.power(adam_first_decay, count), 1.0 - jnp.power(adam_second_decay, count)])
    scales = (
        math.sqrt(max(1.0, hid / feat)),
        math.sqrt(max(1.0, hid / (2 * hid))),
        math.sqrt(max(1.0, classes / hid)),
    )
    norm_rows = (2 * layers, hid)
    smalls = (
        biases,
        norm_params.reshape(norm_rows),
        head_bias[None],
        first_bias,
        first_norm.reshape(norm_rows),
        first_head[None],
        second_bias,
        second_norm.reshape(norm_rows),
        second_head[None],
    )
    outs = update_call(
        n_rows,
        n_batch,
        layers,
        all_nodes,
        rows_at,
        classes,
        NS_PARTS,
        scales,
        pay_rows,
        pay,
        (jnp.pad(full_min, ((0, 0), (0, LANES - feat))), full_mconv, full_mhead),
        (turned[0], w_conv, w_head),
        smalls,
        power,
    )
    loss, new_in, new_conv, new_head, moment_in, moment_conv, moment_head = outs[:7]
    rest = []
    for i in range(0, 9, 3):
        rest += [outs[7 + i], outs[8 + i].reshape(layers, 2, hid), outs[9 + i][0]]
    return (loss[0, 0], new_in.T, new_conv, new_head, moment_in.T, moment_conv, moment_head, *rest)


def solution(mesh):
    in_specs = (
        P("batch", "rows", None),
        P("batch", "rows", None, None),
        P("batch", "rows", None),
        P("batch", "rows", None),
        P("batch", "rows"),
        P("batch", "rows", None, None),
        P(),
        P(None, "batch"),
        P(None, "batch", None),
        P("batch", None),
        P(),
        P(),
        P(),
        P(None, "batch"),
        P(None, "batch", None),
        P("batch", None),
        P(),
        P(),
        P(),
        P(),
        P(),
        P(),
    )
    out_specs = (
        P(),
        P(None, "batch"),
        P(None, "batch", None),
        P("batch", None),
        P(None, "batch"),
        P(None, "batch", None),
        P("batch", None),
        P(),
        P(),
        P(),
        P(),
        P(),
        P(),
        P(),
        P(),
        P(),
    )
    body = functools.partial(per_device, mesh.shape["batch"], mesh.shape["rows"])
    return jax.shard_map(body, mesh=mesh, in_specs=in_specs, out_specs=out_specs, check_vma=False)
```

profile of v0, /device:TPU:0, one launch (start us, length us, event | category | flops | bytes accessed | tf_op | source)
XLA Modules:
  0.0 278.5 jit_solution(12106780383527078267)
XLA Ops:
  0.6 1.0 convert_bitcast_fusion
  1.6 0.7 convert_element_type.40
  2.3 0.7 convert_element_type.42
  3.0 0.1 copy.52
  3.1 0.1 convert_element_type.43
  3.2 0.9 fusion
  4.0 0.7 collective-permute-start.1
  4.7 1.8 collective-permute-start
  6.5 0.8 copy.53.w_head
  7.3 0.8 copy.54
  8.2 0.6 pad.31.refs_12_
  8.8 0.6 pad.32.refs_15_
  9.4 1.3 broadcast_in_dim.15.refs_3_
  10.7 1.2 pad_bitcast_fusion.refs_5_
  12.6 0.7 reshape.86.norms
  13.3 0.7 reshape.87.fn
  14.0 0.7 reshape.88.sn
  14.7 0.1 add_convert_fusion.rims
  14.8 0.1 pad_maximum_fusion.power
  14.8 0.0 collective-permute-done.1
  14.8 0.1 slice.29
  15.0 0.1 reshape.85
  15.1 0.5 pad.30.refs_7_
  15.6 7.1 %order_edges.1 = (s32[128,128]{1,0:T(8,128)S(1)}, f32[128,128]{1,0:T(8,128)S(1)}, bf16[128,128,128]{2,1,0:T(8,128)(2,1)S(1)}, s32[1,128]{1,0:T(1,128)S(1)}, s32[1,128]{1,0:T(1,128)S(1)}) custom-call(f32[128,128]{1,0:T(8,128)S(1)} %get-tuple-element.124.to_ref, f32[128,128]{1,0:T(8,128)S(1)} %get-tuple-element.123.from_ref, ...), custom_call_target="tpu_custom_call" | custom-call | tf_op jit(solution)/shard_map/order_edges/pallas_call | solution.py:118
  22.7 0.0 copy-start
  22.7 2.0 copy-done
  24.7 28.8 %fill_tiles.1 = (bf16[2048,3072]{1,0:T(8,128)(2,1)}, bf16[2048,3072]{1,0:T(8,128)(2,1)}, f32[8,2,128]{2,1,0:T(2,128)S(1)}) custom-call(s32[1,128]{1,0:T(1,128)S(1)} %get-tuple-element.44.lo, s32[1,128]{1,0:T(1,128)S(1)} %get-tuple-element.45.hi, s32[2]{0:T(128)S(1)} %add_convert_fusion.rims, s32[128,128]{1,0:T(8,128)S(1)} %get-tuple-element.46.key_ref, ...), custom_call_target="tpu_custom_call" | custom-call | tf_op jit(solution)/shard_map/fill_tiles/pallas_call | solution.py:215
  53.5 0.6 slice.31.refs_1_
  54.1 0.5 slice_convert_fusion.1.refs_6_
  54.6 0.0 collective-permute-done
  54.6 2.0 copy.51
  56.6 0.0 copy-done.7
  56.6 0.0 copy-start.8
  56.6 0.0 copy-start.9
  56.6 0.0 copy-start.10
  56.6 0.0 copy-start.11
  56.6 0.0 copy-start.12
  56.6 168.5 %forward_backward.1 = (f32[1792,256]{1,0:T(8,128)}, f32[256,100]{1,0:T(8,128)}, f32[3,512,256]{2,1,0:T(8,128)}, f32[256,128]{1,0:T(8,128)}) custom-call(f32[2048,100]{1,0:T(8,128)} %bitcast.37, f32[16,128]{1,0:T(8,128)} %slice.31.refs_1_, f32[8,2,128]{2,1,0:T(2,128)} %copy-done.7, f32[4,1,256]{2,1,0:T(1,128)} %broadcast_in_dim.15.refs_3_, ...), custom_call_target="tpu_custom_call" | custom-call | tf_op jit(solution)/shard_map/forward_backward/pallas_call | solution.py:832
  225.2 0.9 pad.33.mom_in
  226.1 0.0 copy-done.3
  226.1 0.0 copy-done.4
  226.1 0.0 copy-done.6
  226.1 0.0 copy-done.8
  226.1 0.0 copy-done.9
  226.2 0.0 copy-done.10
  226.2 1.5 copy-done.1
  227.7 1.4 copy-done.2
  229.1 0.9 copy-done.5
  230.0 37.6 %sum_and_update.1 = (f32[1,1]{1,0:T(1,128)}, f32[64,100]{1,0:T(8,128)S(1)}, f32[3,128,256]{2,1,0:T(8,128)S(1)}, f32[64,47]{1,0:T(8,128)S(1)}, f32[64,100]{1,0:T(...) custom-call(f32[1792,256]{1,0:T(8,128)S(1)} %copy-done.1, ...), custom_call_target="tpu_custom_call" | custom-call | tf_op jit(solution)/shard_map/sum_and_update/pallas_call | solution.py:1077
  267.6 0.7 copy.56
  268.3 0.7 copy.57
  269.0 0.6 reshape.89
  269.6 0.6 reshape.90
  270.2 0.6 reshape.91
  271.3 0.6 copy.72
  272.0 0.7 copy.73
  272.7 0.6 copy.74
  273.3 0.7 copy.75
  274.1 0.6 copy.76
  274.7 0.5 copy.77
  275.2 0.6 copy.78
  275.8 0.5 copy.79
  276.3 0.6 copy.80
  276.9 0.5 copy.81
  (14 shorter events, 0.1 us)
Async XLA Ops:
  4.0 10.8 %collective-permute-start.1 = (f32[408,128]{1,0:T(8,128)S(1)}, f32[408,128]{1,0:T(8,128)S(1)}, u32[]{:S(2)}, u32[]{:S(2)}) collective-permute-start(f32[408,128]{1,0:T(8,128)S(1)} %fusion), channel_id=1, source_target_pairs={{0,0},{1,8},{2,2},{3,10},{4,4},{5,12},{6,6},{7,14},{8,1},{9,9},{10... | collective-permute-start | bytes 626696 | tf_op jit(solution)/shard_map/ppermute | solution.py:48
  4.7 49.9 %collective-permute-start = (f32[1,2048,100]{1,0,2:T(1,128)}, f32[1,2048,100]{1,0,2:T(1,128)S(1)}, u32[]{:S(2)}, u32[]{:S(2)}) collective-permute-start(f32[1,2048,100]{1,0,2:T(1,128)} %param.22), channel_id=1, source_target_pairs={{0,0},{1,8},{2,2},{3,10},{4,4},{5,12},{6,6},{7,14},{8,1},{9,9},{10... | collective-permute-start | bytes 2457608 | tf_op jit(solution)/shard_map/ppermute | solution.py:48
  22.7 2.0 copy-start
  53.5 3.1 %copy-start.7 = (f32[8,2,128]{2,1,0:T(2,128)}, f32[8,2,128]{2,1,0:T(2,128)S(1)}, u32[]{:S(2)}) copy-start(f32[8,2,128]{2,1,0:T(2,128)S(1)} %get-tuple-element.49.refs_2_) | copy-start | bytes 24580
  56.6 169.5 %copy-start.3 = (f32[3,128,256]{2,1,0:T(8,128)S(1)}, f32[3,128,256]{2,1,0:T(8,128)}, u32[]{:S(2)}) copy-start(f32[3,128,256]{2,1,0:T(8,128)} %w_conv.1) | copy-start | bytes 1179652
  56.6 169.5 %copy-start.4 = (f32[100,64]{0,1:T(8,128)S(1)}, f32[100,64]{0,1:T(8,128)}, u32[]{:S(2)}) copy-start(f32[100,64]{0,1:T(8,128)} %param.28) | copy-start | bytes 76804
  56.6 169.6 %copy-start.6 = (f32[4,256]{1,0:T(4,128)S(1)}, f32[4,256]{1,0:T(4,128)}, u32[]{:S(2)}) copy-start(f32[4,256]{1,0:T(4,128)} %biases.1) | copy-start | bytes 12292
  56.6 169.6 %copy-start.8 = (f32[4,256]{1,0:T(4,128)S(1)}, f32[4,256]{1,0:T(4,128)}, u32[]{:S(2)}) copy-start(f32[4,256]{1,0:T(4,128)} %fb.1) | copy-start | bytes 12292
  56.6 169.6 %copy-start.9 = (f32[4,256]{1,0:T(4,128)S(1)}, f32[4,256]{1,0:T(4,128)}, u32[]{:S(2)}) copy-start(f32[4,256]{1,0:T(4,128)} %sb.1) | copy-start | bytes 12292
  56.6 169.6 %copy-start.10 = (f32[47]{0:T(128)S(1)}, f32[47]{0:T(128)}, u32[]{:S(2)}) copy-start(f32[47]{0:T(128)} %param.33) | copy-start | bytes 568
  56.6 169.6 %copy-start.11 = (f32[47]{0:T(128)S(1)}, f32[47]{0:T(128)}, u32[]{:S(2)}) copy-start(f32[47]{0:T(128)} %param.39) | copy-start | bytes 568
  56.6 169.5 %copy-start.12 = (f32[47]{0:T(128)S(1)}, f32[47]{0:T(128)}, u32[]{:S(2)}) copy-start(f32[47]{0:T(128)} %param.42) | copy-start | bytes 568
  226.2 1.5 copy-start.1
  227.7 1.4 copy-start.2
  229.1 0.9 copy-start.5
where the time goes:
time: 279 us
  Pallas kernels  242 us (87%)
  local copies, waits for them, and re-layouts  26.9 us (10%)
  other arithmetic  3.86 us (1%)
  between operations  3.3 us (1%)
    pallas_call x1, Pallas kernels, step_call(): pl.pallas_call(functools.partial(step_kernel, n, nb, layers, nodes, all_n...  169 us
    pallas_call x1, Pallas kernels, update_call(): pl.pallas_call(functools.partial(update_kernel, n, nb, layers, all_nodes,...  37.6 us
    pallas_call x1, Pallas kernels, fill(): pl.pallas_call(functools.partial(fill_kernel, wide, rim, chunk, parts), o...  28.8 us
    unnamed x41, local copies, waits for them, and re-layouts  14.9 us
    pallas_call x1, Pallas kernels, order_edges(): pl.pallas_call(functools.partial(order_kernel, wide), out_shape=(jax.Shap...  7.08 us
  transfers between devices with their start and end apart: 2, of which 0 were waited for; matrix products, arithmetic and copies ran while one was open for 3% of the time, Pallas kernels for 13%

commit v1 on v0

--- a/solution.py
+++ b/solution.py
@@ -60,7 +60,7 @@
     return peer_place(lax.axis_index("batch"), lax.axis_index("rows"))
 
 
-def order_kernel(wide, to_ref, from_ref, w_ref, key_out, w_out, col_out, lo_out, hi_out):
+def put_in_order(wide, to_ref, from_ref, w_ref, key_out, w_out, col_out, range_out):
     to, frm = to_ref[...].astype(jnp.int32), from_ref[...].astype(jnp.int32)
     key = (((to >> 8) * wide + (frm >> 8)) << 16) | ((to & 255) << 8) | (frm & 255)
     shape3 = (16, 8, LANES)
@@ -105,35 +105,27 @@
         wide_key = wide_key.reshape(shape3)
         below = below + jnp.where(wide_key < start, 1.0, 0.0)
         upto = upto + jnp.where(wide_key < start + 65536.0, 1.0, 0.0)
+    range_out[...] = jnp.zeros_like(range_out)
     n_below = jnp.sum(below.reshape(LANES, LANES), axis=0, keepdims=True)
     n_upto = jnp.sum(upto.reshape(LANES, LANES), axis=0, keepdims=True)
     first = jnp.floor(n_below * (1.0 / 128.0))
     end = jnp.floor((n_upto + 127.0) * (1.0 / 128.0))
-    lo_out[...] = first.astype(jnp.int32)
-    hi_out[...] = jnp.where(n_upto > n_below, end, first).astype(jnp.int32)
-
-
-def order_edges(to, frm, w, wide):
-    vmem = pl.BlockSpec(memory_space=pltpu.VMEM)
-    return pl.pallas_call(
-        functools.partial(order_kernel, wide),
-        out_shape=(
-            jax.ShapeDtypeStruct((LANES, LANES), jnp.int32),
-            jax.ShapeDtypeStruct((LANES, LANES), f32),
-            jax.ShapeDtypeStruct((LANES, LANES, LANES), bf16),
-            jax.ShapeDtypeStruct((1, LANES), jnp.int32),
-            jax.ShapeDtypeStruct((1, LANES), jnp.int32),
-        ),
-        in_specs=[vmem] * 3,
-        out_specs=(vmem,) * 5,
-        compiler_params=pltpu.CompilerParams(vmem_limit_bytes=40 << 20),
-        name="order_edges",
-    )(to, frm, w)
-
-
-def fill_kernel(wide, rim, chunk, parts, lo, hi, rims, key_ref, w_ref, col_ref, *refs):
-    outs, sums, acc, rowacc = refs[:parts], refs[parts], refs[parts + 1], refs[parts + 2]
+    range_out[0:1] = first.astype(jnp.int32)
+    range_out[1:2] = jnp.where(n_upto > n_below, end, first).astype(jnp.int32)
+
+
+def fill_kernel(wide, rim, chunk, parts, rims, to_ref, from_ref, weight_ref, *refs):
+    outs, sums = refs[:parts], refs[parts]
+    acc, rowacc, key_ref, w_ref, col_ref, ranges, span_of, sem = refs[parts + 1 :]
     i = pl.program_id(0)
+
+    @pl.when(i == 0)
+    def _():
+        put_in_order(wide, to_ref, from_ref, weight_ref, key_ref, w_ref, col_ref, ranges)
+        copy = pltpu.make_async_copy(ranges, span_of, sem)
+        copy.start()
+        copy.wait()
+
     pack = 16
     shape = (TILE // pack, pack, LANES)
     rows = lax.broadcasted_iota(jnp.int32, shape, 0) * pack + lax.broadcasted_iota(jnp.int32, shape, 1)
@@ -149,7 +141,7 @@
 
     def tile(j, _):
         b = i * wide + j
-        first, end = lo[0, b], hi[0, b]
+        first, end = span_of[0, b], span_of[1, b]
         end = jnp.where(jnp.logical_and(j < rim, rims[0] == 0), first, end)
         end = jnp.where(jnp.logical_and(j >= wide - rim, rims[1] == 0), first, end)
         slot = jnp.where(j < rim, wide - 2 * rim + j, jnp.where(j < wide - rim, j - rim, j))
@@ -209,25 +201,32 @@
         sums[0, half : half + 1] = column.T[0:1]
 
 
-def fill(order, rims, tiles, wide, rim, parts, chunk=4):
-    key, w, col, lo, hi = order
+def fill(to, frm, weights, rims, tiles, wide, rim, parts, chunk=4):
     cols = wide * TILE
     return pl.pallas_call(
         functools.partial(fill_kernel, wide, rim, chunk, parts),
         out_shape=tuple(jax.ShapeDtypeStruct((tiles * TILE, cols), bf16) for _ in range(parts))
         + (jax.ShapeDtypeStruct((tiles, TILE // LANES, LANES), f32),),
         grid_spec=pltpu.PrefetchScalarGridSpec(
-            num_scalar_prefetch=3,
+            num_scalar_prefetch=1,
             grid=(tiles,),
-            in_specs=[pl.BlockSpec((LANES, LANES), lambda i, *_: (0, 0))] * 2
-            + [pl.BlockSpec((LANES, LANES, LANES), lambda i, *_: (0, 0, 0))],
+            in_specs=[pl.BlockSpec((LANES, LANES), lambda i, *_: (0, 0))] * 3,
             out_specs=tuple(pl.BlockSpec((TILE, cols), lambda i, *_: (i, 0)) for _ in range(parts))
             + (pl.BlockSpec((1, TILE // LANES, LANES), lambda i, *_: (i, 0, 0)),),
-            scratch_shapes=[pltpu.VMEM((TILE, TILE), f32), pltpu.VMEM((TILE, LANES), f32)],
+            scratch_shapes=[
+                pltpu.VMEM((TILE, TILE), f32),
+                pltpu.VMEM((TILE, LANES), f32),
+                pltpu.VMEM((LANES, LANES), jnp.int32),
+                pltpu.VMEM((LANES, LANES), f32),
+                pltpu.VMEM((LANES, LANES, LANES), bf16),
+                pltpu.VMEM((8, LANES), jnp.int32),
+                pltpu.SMEM((8, LANES), jnp.int32),
+                pltpu.SemaphoreType.DMA,
+            ],
         ),
         compiler_params=pltpu.CompilerParams(vmem_limit_bytes=50 << 20),
-        name="fill_tiles",
-    )(lo, hi, rims, key, w, col)
+        name="adjacency_tiles",
+    )(rims, to, frm, weights)
 
 
 def parts_of(x, count):
@@ -306,13 +305,13 @@
 GATHERED = 3
 
 
-def step_kernel(n, nb, layers, nodes, all_nodes, classes, rows_at, summed_rows, *refs):
+def step_kernel(n, nb, layers, nodes, all_nodes, classes, rows_at, summed_rows, label_at, *refs):
     (x_ref, label_ref, sums_ref, bias_ref, norm_ref, head_bias_ref, pick_smem, pick_row, a1_hbm, a2_hbm) = refs[:10]
     own_in, own_conv, own_head, own_min, own_mconv, own_mhead = refs[10:16]
     pay, full_min, full_mconv, full_mhead = refs[16:20]
     (act, agg, a1, a2, p1, p2, g1, g2, gh, rim, out_rim, logit, sent, got, stat, held, w_in, w_conv, w_head,
      wt, a_sem, stat_send, stat_recv, rim_send, rim_recv, pair_send, pair_recv, w_send, w_recv, w_own, sum_send, sum_recv,
-     ready, normed, keep) = refs[20:]
+     ready, normed, keep, stood, laid_head, laid_mhead, wide_bias) = refs[20:]
     rows, width = act.shape[1], act.shape[2]
     halo = rim.shape[2]
     a, ps, gs = (a1, a2), (p1, p2), (g1, g2)
@@ -338,6 +337,12 @@
         span = pl.ds(s * height, height)
         for q, (src, dst) in enumerate(zip((a1_hbm, a2_hbm), a)):
             pltpu.make_async_copy(src.at[span], dst.at[span], a_sem.at[2 * s + q]).start()
+    for src, dst in ((own_head, laid_head), (own_mhead, laid_mhead)):
+        stood[...] = jnp.zeros_like(stood)
+        stood[0:classes] = src[...]
+        dst[...] = stood[...].T
+    wide_bias[...] = jnp.zeros_like(wide_bias)
+    wide_bias[0:1, 0:classes] = head_bias_ref[...]
     pl.semaphore_wait(barrier, n - 1 + nb - 1 + len(places.peers))
 
     def gathers(item, src, dst):
@@ -362,7 +367,7 @@
     in_copies = gather(0, own_in, w_in)
     for q in range(layers):
         gather(2 + q, own_conv.at[q], w_conv.at[q])
-    head_copies = gather(1, own_head, w_head)
+    head_copies = gather(1, laid_head, w_head)
 
     def stat_copies(e):
         return [
@@ -416,7 +421,7 @@
 
     def project(s, _):
         span = rows_of(s, tile)
-        act[0, span] = dots(parts_of(x_ref[span, :], 3), turned_in) + bias_ref[0]
+        act[0, span] = dots(parts_of(x_ref[span, :], 3), turned_in) + bias_ref[0:1]
         return 0
 
     lax.fori_loop(0, tiles, project, 0)
@@ -435,6 +440,8 @@
         normed[l, 2:3] = jnp.where(plain, 1.0, scale)
         normed[l, 3:4] = jnp.where(plain, 0.0, offset)
 
+    bias_row = lax.broadcasted_iota(jnp.int32, bias_ref.shape, 0)
+
     def forward(l, _):
         copies = rims_of(l, act.at[l, pl.ds(0, halo)], act.at[l, pl.ds(rows - halo, halo)])
         start_if(not_first, copies[0])
@@ -484,7 +491,7 @@
         lax.fori_loop(0, rows // height, rims_in, 0)
         arrived(gathers(2 + l, own_conv.at[l], w_conv.at[l]))
         weights = parts_of(w_conv[l], 3)
-        bias = bias_ref[l + 1]
+        bias = column_sums(jnp.where(bias_row == l + 1, bias_ref[...], 0.0))
         scale, offset = normed[l, 2:3], normed[l, 3:4]
 
         def finish(s, sums):
@@ -510,7 +517,7 @@
 
     stats_start(layers)
     base = 2 + layers
-    late = [gather(base, own_min, full_min), gather(base + 1, own_mhead, full_mhead), gather(base + 2, own_mconv, full_mconv)]
+    late = [gather(base, own_min, full_min), gather(base + 1, laid_mhead, full_mhead), gather(base + 2, own_mconv, full_mconv)]
     arrived(head_copies)
     head_parts = parts_of(w_head[...], 3)
     head_turned = parts_of(w_head[...].T, 2)
@@ -523,7 +530,7 @@
 
     def classify(s, _):
         span = rows_of(s, tile)
-        logit[span, :] = dots(parts_of(top(span), 3), head_parts) + head_bias_ref[...]
+        logit[span, :] = dots(parts_of(top(span), 3), head_parts) + wide_bias[0:1]
         return 0
 
     lax.fori_loop(0, tiles, classify, 0)
@@ -549,7 +556,7 @@
         e = jnp.where(real, jnp.exp(z - top_z), 0.0)
         total = jnp.sum(e, axis=1, keepdims=True)
         named = [
-            jnp.broadcast_to(label_ref[pl.ds(s * (tile // LANES) + i, 1), :], (LANES, LANES)).T for i in range(tile // LANES)
+            jnp.broadcast_to(label_ref[pl.ds(label_at + s * (tile // LANES) + i, 1), :], (LANES, LANES)).T for i in range(tile // LANES)
         ]
         hot = jnp.logical_and(real, lane.astype(f32) == jnp.concatenate(named, 0))
         logit[span, :] = e / total - jnp.where(hot, 1.0, 0.0)
@@ -814,7 +821,7 @@
         arrived(copies)
 
 
-def step_call(n, nb, layers, nodes, all_nodes, classes, rows_at, summed_rows, x, labels, sums, biases, norms, head_bias,
+def step_call(n, nb, layers, nodes, all_nodes, classes, rows_at, summed_rows, label_at, x, labels, sums, biases, norms, head_bias,
               picks, pick_row, adjacency, shards):
     rows = x.shape[0]
     width = biases.shape[1]
@@ -830,14 +837,14 @@
     _, ys, across, zs = plane_split(nb, n)
     hops = 2 * ys * across + zs + 1
     return pl.pallas_call(
-        functools.partial(step_kernel, n, nb, layers, nodes, all_nodes, classes, rows_at, summed_rows),
+        functools.partial(step_kernel, n, nb, layers, nodes, all_nodes, classes, rows_at, summed_rows, label_at),
         out_shape=(
             jax.ShapeDtypeStruct((summed_rows + (layers - 1) * 2 * width, width), f32),
             jax.ShapeDtypeStruct((width, feat), f32),
             jax.ShapeDtypeStruct((layers, 2 * width, width), f32),
             jax.ShapeDtypeStruct((width, LANES), f32),
         ),
-        in_specs=[vmem] * 6 + [smem, vmem] + [hbm] * 8,
+        in_specs=[vmem] * 6 + [smem, vmem] + [hbm] * 4 + [vmem] + [hbm] * 2 + [vmem],
         out_specs=(vmem, hbm, hbm, hbm),
         scratch_shapes=[
             pltpu.VMEM((layers + 1, rows, width), f32),
@@ -875,16 +882,20 @@
             pltpu.SemaphoreType.REGULAR((layers - 1,)),
             pltpu.VMEM((layers + 1, 4, width), f32),
             pltpu.VMEM((layers, 4, width), f32),
+            pltpu.VMEM((LANES, width // nb), f32),
+            pltpu.VMEM((width // nb, LANES), f32),
+            pltpu.VMEM((width // nb, LANES), f32),
+            pltpu.VMEM((8, LANES), f32),
         ],
         compiler_params=pltpu.CompilerParams(collective_id=1, has_side_effects=True, vmem_limit_bytes=63 << 20),
         name="forward_backward",
-    )(x, labels, sums, biases[:, None], norms, head_bias, picks, pick_row, *adjacency, *shards)
+    )(x, labels, sums, biases, norms, head_bias, picks, pick_row, *adjacency, *shards)
 
 
 def update_kernel(n, nb, layers, all_nodes, rows_at, classes, ns_parts, scales, summed_rows, pay, mom_in, mom_conv, mom_head, w_in,
                   w_conv, w_head, biases, norms, head_bias, fb, fn, fh, sb, sn, sh, power, *refs):
     (loss_o, in_o, conv_o, head_o, min_o, mconv_o, mhead_o, b_o, n_o, h_o, fb_o, fn_o, fh_o, sb_o, sn_o, sh_o) = refs[:16]
-    (got1, sum1, got2, sum2, got3, full, gram, poly, small_gram, small_poly, mconv, send, recv) = refs[16:]
+    (got1, sum1, got2, sum2, got3, full, gram, poly, small_gram, small_poly, mconv, send, recv, old_conv, old_sem, spread) = refs[16:]
     places = Places(n, nb)
     cores, planes, zs = places.cores, places.planes, places.zs
     core, spot, z = places.core, places.spot, places.z
@@ -925,12 +936,15 @@
             if not late:
                 grams[which[j]] = nxt[j]
 
+    fetch = pltpu.make_async_copy(mom_conv, old_conv, old_sem)
+    fetch.start()
     sizes = {}
     ready = tuple(range(1, layers))
 
     def start_ready():
+        fetch.wait()
         for l in ready:
-            mconv[l] = muon_decay * mom_conv[l] + pay[summed_rows + (l - 1) * 2 * width : summed_rows + l * 2 * width]
+            mconv[l] = muon_decay * old_conv[l] + pay[summed_rows + (l - 1) * 2 * width : summed_rows + l * 2 * width]
             sizes[l] = begin(mconv[l], gram, l)
 
     def middle(count, grams, polys, which):
@@ -1011,13 +1025,15 @@
         mine = part(full, core, half_rows)
         settle([go(mine, mine, core_peer)])
     summed = full[...]
-    mconv[0] = muon_decay * mom_conv[0] + summed[: 2 * width]
+    mconv[0] = muon_decay * old_conv[0] + summed[: 2 * width]
     sizes[0] = begin(mconv[0], gram, 0)
     feat = w_in.shape[1]
     half = width // 2
     grad_in = summed[rows_at[0] : rows_at[0] + LANES].T
     grad_head = summed[rows_at[1] : rows_at[1] + half]
-    moment_in = muon_decay * mom_in[...] + jnp.where(lax.broadcasted_iota(jnp.int32, (width, LANES), 1) < feat, grad_in, 0.0)
+    spread[...] = jnp.zeros_like(spread)
+    spread[:, 0:feat] = mom_in[...]
+    moment_in = muon_decay * spread[...] + jnp.where(lax.broadcasted_iota(jnp.int32, (width, LANES), 1) < feat, grad_in, 0.0)
     moment_head = muon_decay * mom_head[...] + jnp.concatenate([grad_head[:, :LANES], grad_head[:, LANES:]], 0)
     sizes[layers] = begin(moment_in, small_gram, 0)
     sizes[layers + 1] = begin(moment_head, small_gram, 1)
@@ -1038,12 +1054,12 @@
     w = w_in[...]
     turn = kdot(own, small_poly[0]) * (scale_in / sizes[layers])
     in_o[...] = w - muon_rate * (turn[:, :feat] + muon_shrink * w)
-    span = w_head.shape[0]
+    span = w_head.shape[1]
     own = mconv[0, pl.ds(pl.multiple_of(here_b * span, 8), span), LANES : 2 * LANES]
-    mhead_o[...] = own[:, :classes]
+    mhead_o[...] = own.T[:classes]
     w = w_head[...]
     turn = kdot(own, small_poly[1]) * (scale_head / sizes[layers + 1])
-    head_o[...] = w - muon_rate * (turn[:, :classes] + muon_shrink * w)
+    head_o[...] = w - muon_rate * (turn.T[:classes] + muon_shrink * w)
 
     def adamw(param, grad, first, second, outs):
         first = adam_first_decay * first + (1.0 - adam_first_decay) * grad
@@ -1057,7 +1073,9 @@
     at = rows_at[2]
     adamw(biases[...], summed[at : at + layers + 1], fb[...], sb[...], (b_o, fb_o, sb_o))
     at = at + layers + 1
-    adamw(norms[...], summed[at : at + 2 * layers], fn[...], sn[...], (n_o, fn_o, sn_o))
+    for l in range(layers):
+        rows = summed[at + 2 * l : at + 2 * l + 2]
+        adamw(norms[l], rows, fn[l], sn[l], (n_o.at[l], fn_o.at[l], sn_o.at[l]))
     at = at + 2 * layers
     adamw(head_bias[...], summed[at : at + 1, :classes], fh[...], sh[...], (h_o, fh_o, sh_o))
     loss_o[...] = jnp.sum(summed[at + 1 : at + 2], axis=1, keepdims=True) / all_nodes
@@ -1077,7 +1095,7 @@
     return pl.pallas_call(
         functools.partial(update_kernel, n, nb, layers, all_nodes, rows_at, classes, ns_parts, scales, summed_rows),
         out_shape=tuple([jax.ShapeDtypeStruct((1, 1), f32)] + like + like + like_small * 3),
-        in_specs=[vmem] * 16 + [smem],
+        in_specs=[vmem] * 2 + [pl.BlockSpec(memory_space=pl.ANY)] + [vmem] * 13 + [smem],
         out_specs=(vmem,) * 16,
         scratch_shapes=[
             pltpu.VMEM((zs * planes * m, width), f32),
@@ -1093,13 +1111,33 @@
             pltpu.VMEM((layers, 2 * width, width), f32),
             pltpu.SemaphoreType.DMA((copies,)),
             pltpu.SemaphoreType.DMA((copies,)),
+            pltpu.VMEM((layers, 2 * width, width), f32),
+            pltpu.SemaphoreType.DMA,
+            pltpu.VMEM((width, LANES), f32),
         ],
-        compiler_params=pltpu.CompilerParams(collective_id=2, has_side_effects=True, vmem_limit_bytes=48 << 20),
+        compiler_params=pltpu.CompilerParams(collective_id=2, has_side_effects=True, vmem_limit_bytes=63 << 20),
         name="sum_and_update",
     )(pay, *moments, *shards, *smalls, power)
 
 
 NS_PARTS = 3
+
+
+def hand_over_kernel(*refs):
+    half = len(refs) // 2
+    for src, dst in zip(refs[:half], refs[half:]):
+        dst[...] = src[...]
+
+
+def hand_over(arrays):
+    vmem = pl.BlockSpec(memory_space=pltpu.VMEM)
+    return pl.pallas_call(
+        hand_over_kernel,
+        out_shape=tuple(jax.ShapeDtypeStruct(v.shape, v.dtype) for v in arrays),
+        in_specs=[vmem] * len(arrays),
+        out_specs=(vmem,) * len(arrays),
+        name="hand_over",
+    )(*arrays)
 
 
 def per_device(
@@ -1150,10 +1188,8 @@
     block = my_place()[1]
     wide = (rows_dev + 2 * halo_rows) // TILE
     rims = jnp.stack([(block > 0).astype(jnp.int32), (block < n_rows - 1).astype(jnp.int32)])
-    order = order_edges(flat[:e], flat[e : 2 * e], flat[2 * e : 3 * e], wide)
-    *adjacency, row_sums = fill(order, rims, rows_dev // TILE, wide, halo_rows // TILE, 2)
+    *adjacency, row_sums = fill(flat[:e], flat[e : 2 * e], flat[2 * e : 3 * e], rims, rows_dev // TILE, wide, halo_rows // TILE, 2)
     label_rows = rows_dev // LANES
-    node_labels = flat[3 * e : 3 * e + label_rows]
     picks = flat[3 * e + label_rows :].reshape(-1)[: n_rows * pairs].astype(jnp.int32)
     spread = jnp.pad(picks.reshape(n_rows, pairs), ((0, 0), (0, 8 - pairs)), constant_values=-1).reshape(1, n_rows * 8)
     spread = jnp.pad(spread, ((0, 0), (0, -spread.shape[1] % LANES)), constant_values=-1)
@@ -1167,10 +1203,10 @@
     turned = [
         w_in.T,
         w_conv,
-        jnp.pad(w_head, ((0, 0), (0, LANES - classes))),
+        w_head.T,
         mom_in.T,
         mom_conv,
-        jnp.pad(mom_head, ((0, 0), (0, LANES - classes))),
+        mom_head.T,
     ]
     pay, full_min, full_mconv, full_mhead = step_call(
         n_rows,
@@ -1181,12 +1217,13 @@
         classes,
         rows_at,
         pay_rows,
+        3 * e,
         inputs,
-        node_labels,
+        flat,
         row_sums,
         biases,
         norm_params,
-        jnp.pad(head_bias, (0, LANES - classes))[None],
+        head_bias[None],
         picks,
         spread,
         adjacency,
@@ -1199,16 +1236,15 @@
         math.sqrt(max(1.0, hid / (2 * hid))),
         math.sqrt(max(1.0, classes / hid)),
     )
-    norm_rows = (2 * layers, hid)
     smalls = (
         biases,
-        norm_params.reshape(norm_rows),
+        norm_params,
         head_bias[None],
         first_bias,
-        first_norm.reshape(norm_rows),
+        first_norm,
         first_head[None],
         second_bias,
-        second_norm.reshape(norm_rows),
+        second_norm,
         second_head[None],
     )
     outs = update_call(
@@ -1222,16 +1258,17 @@
         scales,
         pay_rows,
         pay,
-        (jnp.pad(full_min, ((0, 0), (0, LANES - feat))), full_mconv, full_mhead),
-        (turned[0], w_conv, w_head),
+        (full_min, full_mconv, full_mhead),
+        (turned[0], w_conv, turned[2]),
         smalls,
         power,
     )
+    outs = hand_over(outs)
     loss, new_in, new_conv, new_head, moment_in, moment_conv, moment_head = outs[:7]
     rest = []
     for i in range(0, 9, 3):
-        rest += [outs[7 + i], outs[8 + i].reshape(layers, 2, hid), outs[9 + i][0]]
-    return (loss[0, 0], new_in.T, new_conv, new_head, moment_in.T, moment_conv, moment_head, *rest)
+        rest += [outs[7 + i], outs[8 + i], outs[9 + i][0]]
+    return (loss[0, 0], new_in.T, new_conv, new_head.T, moment_in.T, moment_conv, moment_head.T, *rest)
 
 
 def solution(mesh):

time: 279 us -> 258 us (0.925)
  local copies, waits for them, and re-layouts: 26.9 us -> 3.47 us
  Pallas kernels: 242 us -> 245 us
    unnamed x41 -> x5, local copies, waits for them, and re-layouts: 14.9 us -> 0.61 us
    pallas_call x1, Pallas kernels: 28.8 us -> 33.4 us  [fill(): pl.pallas_call(functools.partial(fill_kernel, wide, rim, chunk, parts), o...]
    pallas_call x1, Pallas kernels: 7.08 us -> 2.74 us  [hand_over(): pl.pallas_call(hand_over_kernel, out_shape=tuple((jax.ShapeDtypeStruct(v....]
    reshape x6 -> x0, local copies, waits for them, and re-layouts: 3.9 us -> none  [the longest x3 1.8 us: per_device(): rest += [outs[7 + i], outs[8 + i].reshape(layers, 2, hid), outs[9 + i][0]]]
  transfers between devices with their start and end apart: 2 -> 2, of which waited for: 0 -> 0; matrix products, arithmetic and copies ran while one was open for 3% -> 1% of each run, Pallas kernels for 13% -> 13%
where the time goes in v1:
time: 258 us; the launch traced here: 257 us
  Pallas kernels  245 us (95%)
  other arithmetic  4.37 us (2%)
  local copies, waits for them, and re-layouts  3.47 us (1%)
    pallas_call x1, Pallas kernels, step_call(): pl.pallas_call(functools.partial(step_kernel, n, nb, layers, nodes, all_n...  169 us
    pallas_call x1, Pallas kernels, update_call(): pl.pallas_call(functools.partial(update_kernel, n, nb, layers, all_nodes,...  40 us
    pallas_call x1, Pallas kernels, fill(): pl.pallas_call(functools.partial(fill_kernel, wide, rim, chunk, parts), o...  33.4 us
  transfers between devices with their start and end apart: 2, of which 0 were waited for; matrix products, arithmetic and copies ran while one was open for 1% of the time, Pallas kernels for 13%

profile of v1, /device:TPU:0, one launch (start us, length us, event | category | flops | bytes accessed | tf_op | source)
XLA Modules:
  0.0 257.1 jit_solution(17405312391303204458)
XLA Ops:
  0.6 1.0 convert_bitcast_fusion
  1.6 0.7 convert_element_type.33
  2.3 0.7 convert_element_type.35
  3.0 0.1 copy.42
  3.1 0.1 convert_element_type.36
  3.2 0.9 fusion
  4.0 0.7 collective-permute-start.1
  4.7 1.8 collective-permute-start
  7.3 0.1 add_convert_fusion.rims
  7.3 0.6 pad_maximum_fusion.power
  7.9 0.0 collective-permute-done.1.refs_1_
  7.9 0.0 copy-start.1
  7.9 0.1 slice.25
  8.1 0.1 reshape.67
  8.2 0.5 pad.14.refs_7_
  8.7 33.4 %adjacency_tiles.1 = (bf16[2048,3072]{1,0:T(8,128)(2,1)}, bf16[2048,3072]{1,0:T(8,128)(2,1)}, f32[8,2,128]{2,1,0:T(2,128)S(1)}) custom-call(s32[2]{0:T(128)S(1)} %add_convert_fusion.rims, f32[128,128]{1,0:T(8,128)S(1)} %get-tuple-element.98.to_ref, f32[128,128]{1,0:T(8,128)S(1)} %get-tuple-element.97.from_ref, f32[128,128]{1,0:T(8,128)S(1)} %get-tuple-element.96.weight_ref), custom_call_target="tpu_custom_call" | custom-call | tf_op jit(solution)/shard_map/adjacency_tiles/pallas_call | solution.py:206
  42.1 0.0 copy-start
  42.1 0.6 copy-done
  42.7 0.5 slice_convert_fusion.1.refs_6_
  43.2 0.0 collective-permute-done
  43.2 1.9 copy.41
  45.2 0.0 copy-done.1
  45.2 169.0 %forward_backward.1 = (f32[1792,256]{1,0:T(8,128)}, f32[256,100]{1,0:T(8,128)}, f32[3,512,256]{2,1,0:T(8,128)}, f32[256,128]{1,0:T(8,128)}) custom-call(f32[2048,100]{1,0:T(8,128)} %bitcast.29, f32[408,128]{1,0:T(8,128)} %copy-done.1, f32[8,2,128]{2,1,0:T(2,128)} %copy-done, f32[4,256]{1,0:T(4,128)} %biases.1, f32[3,2,256]{2,1,0:T(2,128)} %norms.1, ...), custom_call_target="tpu_custom_call" | custom-call | tf_op jit(solution)/shard_map/forward_backward/pallas_call | solution.py:839
  214.2 40.0 %sum_and_update.1 = (f32[1,1]{1,0:T(1,128)}, f32[64,100]{1,0:T(8,128)}, f32[3,128,256]{2,1,0:T(8,128)}, f32[47,64]{1,0:T(8,128)}, f32[64,100]{1,0:T(8,128)}, /*i...) custom-call(f32[1792,256]{1,0:T(8,128)} %get-tuple-element.58.pay, ...), custom_call_target="tpu_custom_call" | custom-call | tf_op jit(solution)/shard_map/sum_and_update/pallas_call | solution.py:1095
  254.2 2.7 %hand_over.1 = (f32[1,1]{1,0:T(1,128)}, f32[64,100]{1,0:T(8,128)}, f32[3,128,256]{2,1,0:T(8,128)}, f32[47,64]{1,0:T(8,128)}, f32[64,100]{1,0:T(8,128)}, /*index=...) custom-call(f32[1,1]{1,0:T(1,128)} %get-tuple-element.62.refs_0_, ...), custom_call_target="tpu_custom_call" | custom-call | tf_op jit(solution)/shard_map/hand_over/pallas_call | solution.py:1134
  (5 shorter events, 0.0 us)
Async XLA Ops:
  4.0 3.9 %collective-permute-start.1 = (f32[408,128]{1,0:T(8,128)S(1)}, f32[408,128]{1,0:T(8,128)S(1)}, u32[]{:S(2)}, u32[]{:S(2)}) collective-permute-start(f32[408,128]{1,0:T(8,128)S(1)} %fusion), channel_id=1, source_target_pairs={{0,0},{1,8},{2,2},{3,10},{4,4},{5,12},{6,6},{7,14},{8,1},{9,9},{10... | collective-permute-start | bytes 626696 | tf_op jit(solution)/shard_map/ppermute | solution.py:48
  4.7 38.5 %collective-permute-start = (f32[1,2048,100]{1,0,2:T(1,128)}, f32[1,2048,100]{1,0,2:T(1,128)S(1)}, u32[]{:S(2)}, u32[]{:S(2)}) collective-permute-start(f32[1,2048,100]{1,0,2:T(1,128)} %param.22), channel_id=1, source_target_pairs={{0,0},{1,8},{2,2},{3,10},{4,4},{5,12},{6,6},{7,14},{8,1},{9,9},{10... | collective-permute-start | bytes 2457608 | tf_op jit(solution)/shard_map/ppermute | solution.py:48
  7.9 37.3 %copy-start.1 = (f32[408,128]{1,0:T(8,128)}, f32[408,128]{1,0:T(8,128)S(1)}, u32[]{:S(2)}) copy-start(f32[408,128]{1,0:T(8,128)S(1)} %collective-permute-done.1.refs_1_) | copy-start | bytes 626692
  42.1 0.6 copy-start

commit v2 on v1

--- a/solution.py
+++ b/solution.py
@@ -421,7 +421,10 @@
 
     def project(s, _):
         span = rows_of(s, tile)
-        act[0, span] = dots(parts_of(x_ref[span, :], 3), turned_in) + bias_ref[0:1]
+        h = dots(parts_of(x_ref[span, :], 3), turned_in) + bias_ref[0:1]
+        act[0, span] = h
+        for dst, piece in zip(ps, parts_of(h, 2)):
+            dst[span, :] = piece
         return 0
 
     lax.fori_loop(0, tiles, project, 0)
@@ -448,14 +451,6 @@
         start_if(not_last, copies[1])
         stats_start(l)
 
-        def split(s, _):
-            span = rows_of(s, tile)
-            for dst, piece in zip(ps, parts_of(act[l, span], 2)):
-                dst[span, :] = piece
-            return 0
-
-        lax.fori_loop(0, tiles, split, 0)
-
         def own(s, _):
             span = rows_of(s, height)
 
@@ -505,6 +500,8 @@
             pre = dots(parts_of(jnp.concatenate([h, found], 1), 3), weights) + bias
             active = jnp.maximum(pre, 0.0)
             act[l + 1, span] = active
+            for dst, piece in zip(ps, parts_of(active, 2)):
+                dst[span, :] = piece
             return sums[0] + folded(active), sums[1] + folded(active * active)
 
         sums = lax.fori_loop(0, tiles, finish, (zeros8, zeros8))
@@ -631,6 +628,8 @@
     core, spot = places.core, places.spot
     piece_rows = big // cores
     block_rows = piece_rows // planes
+    cut = block_rows % (8 * zs) == 0
+    slice_rows = block_rows // zs if cut else block_rows
 
     def part(ref, index, count):
         return ref.at[pl.ds(pl.multiple_of(index * count, 8), count)]
@@ -640,7 +639,7 @@
             self.which, room = l - 1, act.at[l + 1]
             self.local = pay.at[pl.ds(conv_rows(l), big)]
             self.whole = room.at[pl.ds(0, big)]
-            spots = [piece_rows, piece_rows, piece_rows, block_rows, block_rows * zs]
+            spots = [piece_rows, piece_rows, piece_rows, block_rows, slice_rows * zs]
             views, at = [], big
             for count in spots:
                 views.append(room.at[pl.ds(at, count)])
@@ -661,14 +660,20 @@
                     add(k, part(self.sum1, p, block_rows), part(self.got2, k, block_rows), to)
             if stage == 2:
                 for k in range(1, zs):
-                    add(planes + k, self.sum2, part(self.got3, k, block_rows), places.column_peer(k)[1])
-            if stage == 3:
-                mine = part(self.whole, core * planes + spot, block_rows)
+                    q, to = places.column_peer(k)
+                    src = part(self.sum2, q, slice_rows) if cut else self.sum2
+                    add(planes + k, src, part(self.got3, k, slice_rows), to)
+            block = part(self.whole, core * planes + spot, block_rows)
+            if stage == 3 and cut:
+                mine = part(self.whole, (core * planes + spot) * zs + places.z, slice_rows)
+                for k in range(1, zs):
+                    add(planes + zs + k, mine, mine, places.column_peer(k)[1])
+            if stage == 4:
                 for k in range(1, planes):
-                    add(planes + zs + k, mine, mine, places.plane_peer(k)[1])
-            if stage == 4 and cores == 2:
+                    add(planes + 2 * zs + k, block, block, places.plane_peer(k)[1])
+            if stage == 5 and cores == 2:
                 mine = part(self.whole, core, piece_rows)
-                add(2 * planes + zs, mine, mine, places.core_peer)
+                add(2 * planes + 2 * zs, mine, mine, places.core_peer)
             return found
 
         def go(self, stage):
@@ -686,13 +691,16 @@
                 for k in range(1, planes):
                     total = total + part(self.got2, k, block_rows)[...]
                 self.sum2[...] = total
-                self.got3[pl.ds(0, block_rows), :] = total
+                self.got3[pl.ds(0, slice_rows), :] = part(self.sum2, places.z, slice_rows)[...] if cut else total
             if stage == 3:
-                total = part(self.got3, lax.rem(places.z, zs), block_rows)[...]
+                total = part(self.got3, lax.rem(places.z, zs), slice_rows)[...]
                 for q in range(1, zs):
-                    total = total + part(self.got3, lax.rem(places.z + zs - q, zs), block_rows)[...]
-                part(self.whole, core * planes + spot, block_rows)[...] = total
-            if stage == 5:
+                    total = total + part(self.got3, lax.rem(places.z + zs - q, zs), slice_rows)[...]
+                if cut:
+                    part(self.whole, (core * planes + spot) * zs + places.z, slice_rows)[...] = total
+                else:
+                    part(self.whole, core * planes + spot, block_rows)[...] = total
+            if stage == 6:
                 self.local[...] = self.whole[...]
             for copy in self.copies(stage):
                 copy.start()
@@ -737,6 +745,11 @@
             told(l - 1)
 
         advance(1)
+
+        @pl.when(turn > 1)
+        def _():
+            Sum(l + 2).go(6)
+
         copies = rims_of(e, out_rim.at[0], out_rim.at[1])
 
         def rims_out(which, _):
@@ -752,10 +765,15 @@
         def spread_back(s, _):
             span = rows_of(s, height)
             gh[span, :] += dots([q[:, span] for q in a], [q[own_cols, :] for q in ps], TURNED)
+
+            @pl.when(jnp.logical_and(turn > 0, s == rows // height // 2))
+            def _():
+                Sum(l + 1).go(3)
+
             return 0
 
         lax.fori_loop(0, rows // height, spread_back, 0)
-        advance(3)
+        advance(4)
         slot = lax.rem(e, 2)
         for which, go, start in ((1, not_last, rows - halo), (0, not_first, 0)):
             @pl.when(go)
@@ -780,7 +798,6 @@
             stats_start(e + 1)
 
         rims_sent(copies)
-        advance(4)
         base = conv_rows(l)
         where = pl.ds(base, width)
         under = pl.ds(pl.multiple_of(base + width, 8), width)
@@ -819,6 +836,8 @@
     pay[pl.ds(rows_at[0], feat), :] = lax.fori_loop(0, rows // height, weigh_in, jnp.zeros((feat, width), f32))
     for copies in late:
         arrived(copies)
+    if layers > 1:
+        Sum(1).go(6)
 
 
 def step_call(n, nb, layers, nodes, all_nodes, classes, rows_at, summed_rows, label_at, x, labels, sums, biases, norms, head_bias,
@@ -835,7 +854,7 @@
     items = 2 + layers + 3
     exchanges = 2 * layers + 1
     _, ys, across, zs = plane_split(nb, n)
-    hops = 2 * ys * across + zs + 1
+    hops = 2 * ys * across + 2 * zs + 1
     return pl.pallas_call(
         functools.partial(step_kernel, n, nb, layers, nodes, all_nodes, classes, rows_at, summed_rows, label_at),
         out_shape=(

time: 258 us -> 254 us (0.984)
  Pallas kernels: 245 us -> 242 us
    pallas_call x1, Pallas kernels: 169 us -> 166 us  [step_call(): pl.pallas_call(functools.partial(step_kernel, n, nb, layers, nodes, all_n...]
  transfers between devices with their start and end apart: 2 -> 2, of which waited for: 0 -> 0; matrix products, arithmetic and copies ran while one was open for 1% -> 1% of each run, Pallas kernels for 13% -> 14%
where the time goes in v2:
time: 254 us
  Pallas kernels  242 us (95%)
  other arithmetic  4.37 us (2%)
  local copies, waits for them, and re-layouts  3.47 us (1%)
    pallas_call x1, Pallas kernels, step_call(): pl.pallas_call(functools.partial(step_kernel, n, nb, layers, nodes, all_n...  166 us
    pallas_call x1, Pallas kernels, update_call(): pl.pallas_call(functools.partial(update_kernel, n, nb, layers, all_nodes,...  38.6 us
    pallas_call x1, Pallas kernels, fill(): pl.pallas_call(functools.partial(fill_kernel, wide, rim, chunk, parts), o...  34.3 us
  transfers between devices with their start and end apart: 2, of which 0 were waited for; matrix products, arithmetic and copies ran while one was open for 1% of the time, Pallas kernels for 14%

profile of v2, /device:TPU:0, one launch (start us, length us, event | category | flops | bytes accessed | tf_op | source)
XLA Modules:
  0.0 253.7 jit_solution(3282892703719253196)
XLA Ops:
  0.6 1.0 convert_bitcast_fusion
  1.6 0.7 convert_element_type.33
  2.3 0.7 convert_element_type.35
  3.0 0.1 copy.42
  3.1 0.1 convert_element_type.36
  3.2 0.9 fusion
  4.0 0.7 collective-permute-start.1
  4.7 1.8 collective-permute-start
  7.3 0.1 add_convert_fusion.rims
  7.3 0.6 pad_maximum_fusion.power
  7.9 0.0 collective-permute-done.1.refs_1_
  7.9 0.0 copy-start.1
  7.9 0.1 slice.25
  8.1 0.1 reshape.67
  8.2 0.5 pad.14.refs_7_
  8.7 34.3 %adjacency_tiles.1 = (bf16[2048,3072]{1,0:T(8,128)(2,1)}, bf16[2048,3072]{1,0:T(8,128)(2,1)}, f32[8,2,128]{2,1,0:T(2,128)S(1)}) custom-call(s32[2]{0:T(128)S(1)} %add_convert_fusion.rims, f32[128,128]{1,0:T(8,128)S(1)} %get-tuple-element.98.to_ref, f32[128,128]{1,0:T(8,128)S(1)} %get-tuple-element.97.from_ref, f32[128,128]{1,0:T(8,128)S(1)} %get-tuple-element.96.weight_ref), custom_call_target="tpu_custom_call" | custom-call | tf_op jit(solution)/shard_map/adjacency_tiles/pallas_call | solution.py:206
  43.0 0.0 copy-start
  43.0 0.6 copy-done
  43.6 0.5 slice_convert_fusion.1.refs_6_
  44.1 0.0 collective-permute-done
  44.1 1.9 copy.41
  46.1 0.0 copy-done.1
  46.1 166.1 %forward_backward.1 = (f32[1792,256]{1,0:T(8,128)}, f32[256,100]{1,0:T(8,128)}, f32[3,512,256]{2,1,0:T(8,128)}, f32[256,128]{1,0:T(8,128)}) custom-call(f32[2048,100]{1,0:T(8,128)} %bitcast.29, f32[408,128]{1,0:T(8,128)} %copy-done.1, f32[8,2,128]{2,1,0:T(2,128)} %copy-done, f32[4,256]{1,0:T(4,128)} %biases.1, f32[3,2,256]{2,1,0:T(2,128)} %norms.1, ...), custom_call_target="tpu_custom_call" | custom-call | tf_op jit(solution)/shard_map/forward_backward/pallas_call | solution.py:858
  212.1 38.6 %sum_and_update.1 = (f32[1,1]{1,0:T(1,128)}, f32[64,100]{1,0:T(8,128)}, f32[3,128,256]{2,1,0:T(8,128)}, f32[47,64]{1,0:T(8,128)}, f32[64,100]{1,0:T(8,128)}, /*i...) custom-call(f32[1792,256]{1,0:T(8,128)} %get-tuple-element.58.pay, ...), custom_call_target="tpu_custom_call" | custom-call | tf_op jit(solution)/shard_map/sum_and_update/pallas_call | solution.py:1114
  250.7 2.7 %hand_over.1 = (f32[1,1]{1,0:T(1,128)}, f32[64,100]{1,0:T(8,128)}, f32[3,128,256]{2,1,0:T(8,128)}, f32[47,64]{1,0:T(8,128)}, f32[64,100]{1,0:T(8,128)}, /*index=...) custom-call(f32[1,1]{1,0:T(1,128)} %get-tuple-element.62.refs_0_, ...), custom_call_target="tpu_custom_call" | custom-call | tf_op jit(solution)/shard_map/hand_over/pallas_call | solution.py:1153
  (5 shorter events, 0.0 us)
Async XLA Ops:
  4.0 3.9 %collective-permute-start.1 = (f32[408,128]{1,0:T(8,128)S(1)}, f32[408,128]{1,0:T(8,128)S(1)}, u32[]{:S(2)}, u32[]{:S(2)}) collective-permute-start(f32[408,128]{1,0:T(8,128)S(1)} %fusion), channel_id=1, source_target_pairs={{0,0},{1,8},{2,2},{3,10},{4,4},{5,12},{6,6},{7,14},{8,1},{9,9},{10... | collective-permute-start | bytes 626696 | tf_op jit(solution)/shard_map/ppermute | solution.py:48
  4.7 39.4 %collective-permute-start = (f32[1,2048,100]{1,0,2:T(1,128)}, f32[1,2048,100]{1,0,2:T(1,128)S(1)}, u32[]{:S(2)}, u32[]{:S(2)}) collective-permute-start(f32[1,2048,100]{1,0,2:T(1,128)} %param.22), channel_id=1, source_target_pairs={{0,0},{1,8},{2,2},{3,10},{4,4},{5,12},{6,6},{7,14},{8,1},{9,9},{10... | collective-permute-start | bytes 2457608 | tf_op jit(solution)/shard_map/ppermute | solution.py:48
  7.9 38.2 %copy-start.1 = (f32[408,128]{1,0:T(8,128)}, f32[408,128]{1,0:T(8,128)S(1)}, u32[]{:S(2)}) copy-start(f32[408,128]{1,0:T(8,128)S(1)} %collective-permute-done.1.refs_1_) | copy-start | bytes 626692
  43.0 0.6 copy-start

commit v3 on v2

--- a/solution.py
+++ b/solution.py
@@ -201,7 +201,7 @@
         sums[0, half : half + 1] = column.T[0:1]
 
 
-def fill(to, frm, weights, rims, tiles, wide, rim, parts, chunk=4):
+def fill(to, frm, weights, rims, tiles, wide, rim, parts, chunk=5):
     cols = wide * TILE
     return pl.pallas_call(
         functools.partial(fill_kernel, wide, rim, chunk, parts),
@@ -333,10 +333,19 @@
     for peer in places.peers:
         pl.semaphore_signal(barrier, inc=1, device_id=peer, device_id_type=pl.DeviceIdType.MESH)
     height = 512
-    for s in range(rows // height):
-        span = pl.ds(s * height, height)
-        for q, (src, dst) in enumerate(zip((a1_hbm, a2_hbm), a)):
-            pltpu.make_async_copy(src.at[span], dst.at[span], a_sem.at[2 * s + q]).start()
+    steps = rows // height
+    own_cols, rim_cols = pl.ds(0, rows), pl.ds(rows, 2 * halo)
+
+    def load(s, cols, which):
+        span = pl.ds(pl.multiple_of(s * height, height), height)
+        return [
+            pltpu.make_async_copy(src.at[span, cols], dst.at[span, cols], a_sem.at[2 * (steps * which + s) + q])
+            for q, (src, dst) in enumerate(zip((a1_hbm, a2_hbm), a))
+        ]
+
+    for s in range(steps):
+        for copy in load(s, own_cols, 0):
+            copy.start()
     for src, dst in ((own_head, laid_head), (own_mhead, laid_mhead)):
         stood[...] = jnp.zeros_like(stood)
         stood[0:classes] = src[...]
@@ -429,8 +438,6 @@
 
     lax.fori_loop(0, tiles, project, 0)
     stat[0] = jnp.zeros((2, width), f32)
-    own_cols, rim_cols = pl.ds(0, rows), pl.ds(rows, 2 * halo)
-
     def set_norm(l, totals):
         mean = totals[0:1] * (1.0 / nodes)
         inverse = lax.rsqrt(totals[1:2] * (1.0 / nodes) - mean * mean + norm_epsilon)
@@ -456,8 +463,10 @@
 
             @pl.when(l == 0)
             def _():
-                for q, (src, dst) in enumerate(zip((a1_hbm, a2_hbm), a)):
-                    pltpu.make_async_copy(src.at[span], dst.at[span], a_sem.at[2 * s + q]).wait()
+                for copy in load(s, own_cols, 0):
+                    copy.wait()
+                for copy in load(s, rim_cols, 1):
+                    copy.start()
 
             agg[l, span] = dots([q[span, own_cols] for q in a], [q[own_cols, :] for q in ps])
             return 0
@@ -480,6 +489,12 @@
 
         def rims_in(s, _):
             span = rows_of(s, height)
+
+            @pl.when(l == 0)
+            def _():
+                for copy in load(s, rim_cols, 1):
+                    copy.wait()
+
             agg[l, span] += dots([q[span, rim_cols] for q in a], [q[rim_cols, :] for q in ps])
             return 0
 
@@ -748,7 +763,7 @@
 
         @pl.when(turn > 1)
         def _():
-            Sum(l + 2).go(6)
+            Sum(l + 2).go(5)
 
         copies = rims_of(e, out_rim.at[0], out_rim.at[1])
 
@@ -762,18 +777,17 @@
         lax.fori_loop(0, 2, rims_out, 0)
         advance(2)
 
+        @pl.when(turn > 1)
+        def _():
+            Sum(l + 2).go(6)
+
         def spread_back(s, _):
             span = rows_of(s, height)
             gh[span, :] += dots([q[:, span] for q in a], [q[own_cols, :] for q in ps], TURNED)
-
-            @pl.when(jnp.logical_and(turn > 0, s == rows // height // 2))
-            def _():
-                Sum(l + 1).go(3)
-
             return 0
 
         lax.fori_loop(0, rows // height, spread_back, 0)
-        advance(4)
+        advance(3)
         slot = lax.rem(e, 2)
         for which, go, start in ((1, not_last, rows - halo), (0, not_first, 0)):
             @pl.when(go)
@@ -798,6 +812,7 @@
             stats_start(e + 1)
 
         rims_sent(copies)
+        advance(4)
         base = conv_rows(l)
         where = pl.ds(base, width)
         under = pl.ds(pl.multiple_of(base + width, 8), width)
@@ -813,7 +828,6 @@
             return 0
 
         lax.fori_loop(0, rows // height, weigh, 0)
-        advance(5)
 
         @pl.when(l > 0)
         def _():
@@ -834,6 +848,8 @@
         return total + dots(parts_of(x_ref[span, :], 2), parts_of(gh[span, :], 2), TURNED)
 
     pay[pl.ds(rows_at[0], feat), :] = lax.fori_loop(0, rows // height, weigh_in, jnp.zeros((feat, width), f32))
+    if layers > 1:
+        Sum(1).go(5)
     for copies in late:
         arrived(copies)
     if layers > 1:
@@ -886,7 +902,7 @@
             pltpu.VMEM((layers, 2 * width, width), f32),
             pltpu.VMEM((width, LANES), f32),
             pltpu.VMEM((2, width, 2 * width), bf16),
-            dma((2 * rows // 512,)),
+            dma((4 * rows // 512,)),
             dma((exchanges, n)),
             dma((exchanges, n)),
             dma((exchanges, 2)),
@@ -940,16 +956,22 @@
     def step(grams, polys, which, early, late):
         k = grams.shape[1]
         count = len(which)
+        def split(values):
+            return [parts_of(v, ns_parts) for v in values]
+
         a1 = [grams[i] for i in which]
-        a2 = [kdot(v, v) for v in a1]
+        a1_parts = split(a1)
+        a2 = [dots(v, v) for v in a1_parts]
         p = [newton_a * eye(k) + newton_b * v + newton_c * u for v, u in zip(a1, a2)]
+        p_parts = split(p)
+        if not late:
+            pa = [dots(v, u) for v, u in zip(p_parts, a1_parts)]
         if early:
             q = p
         else:
-            q = [kdot(v, polys[i]) for i, v in zip(which, p)]
+            q = [dots(v, parts_of(polys[i], ns_parts)) for i, v in zip(which, p_parts)]
         if not late:
-            pa = [kdot(v, u) for v, u in zip(p, a1)]
-            nxt = [kdot(v, u) for v, u in zip(pa, p)]
+            nxt = [dots(v, u) for v, u in zip(split(pa), p_parts)]
         for j in range(count):
             polys[which[j]] = q[j]
             if not late:

time: 254 us -> 247 us (0.972)
  Pallas kernels: 242 us -> 234 us
    pallas_call x1, Pallas kernels: 34.3 us -> 30.7 us  [fill(): pl.pallas_call(functools.partial(fill_kernel, wide, rim, chunk, parts), o...]
    pallas_call x1, Pallas kernels: 166 us -> 163 us  [step_call(): pl.pallas_call(functools.partial(step_kernel, n, nb, layers, nodes, all_n...]
  transfers between devices with their start and end apart: 2 -> 2, of which waited for: 0 -> 0; matrix products, arithmetic and copies ran while one was open for 1% -> 1% of each run, Pallas kernels for 14% -> 12%
where the time goes in v3:
time: 247 us; the launch traced here: 246 us
  Pallas kernels  234 us (95%)
  other arithmetic  4.37 us (2%)
  local copies, waits for them, and re-layouts  3.47 us (1%)
  starting transfers between devices  2.48 us (1%)
    pallas_call x1, Pallas kernels, step_call(): pl.pallas_call(functools.partial(step_kernel, n, nb, layers, nodes, all_n...  163 us
    pallas_call x1, Pallas kernels, update_call(): pl.pallas_call(functools.partial(update_kernel, n, nb, layers, all_nodes,...  38.3 us
    pallas_call x1, Pallas kernels, fill(): pl.pallas_call(functools.partial(fill_kernel, wide, rim, chunk, parts), o...  30.7 us
  transfers between devices with their start and end apart: 2, of which 0 were waited for; matrix products, arithmetic and copies ran while one was open for 1% of the time, Pallas kernels for 12%

profile of v3, /device:TPU:0, one launch (start us, length us, event | category | flops | bytes accessed | tf_op | source)
XLA Modules:
  0.0 246.3 jit_solution(1129686263673092413)
XLA Ops:
  0.6 1.0 convert_bitcast_fusion
  1.6 0.7 convert_element_type.33
  2.3 0.7 convert_element_type.35
  3.0 0.1 copy.42
  3.1 0.1 convert_element_type.36
  3.2 0.9 fusion
  4.0 0.7 collective-permute-start.1
  4.7 1.8 collective-permute-start
  7.3 0.1 add_convert_fusion.rims
  7.3 0.6 pad_maximum_fusion.power
  7.9 0.0 collective-permute-done.1.refs_1_
  7.9 0.0 copy-start.1
  7.9 0.1 slice.25
  8.1 0.1 reshape.67
  8.2 0.5 pad.14.refs_7_
  8.7 30.7 %adjacency_tiles.1 = (bf16[2048,3072]{1,0:T(8,128)(2,1)}, bf16[2048,3072]{1,0:T(8,128)(2,1)}, f32[8,2,128]{2,1,0:T(2,128)S(1)}) custom-call(s32[2]{0:T(128)S(1)} %add_convert_fusion.rims, f32[128,128]{1,0:T(8,128)S(1)} %get-tuple-element.98.to_ref, f32[128,128]{1,0:T(8,128)S(1)} %get-tuple-element.97.from_ref, f32[128,128]{1,0:T(8,128)S(1)} %get-tuple-element.96.weight_ref), custom_call_target="tpu_custom_call" | custom-call | tf_op jit(solution)/shard_map/adjacency_tiles/pallas_call | solution.py:206
  39.4 0.0 copy-start
  39.4 0.6 copy-done
  40.0 0.5 slice_convert_fusion.1.refs_6_
  40.5 0.0 collective-permute-done
  40.5 1.9 copy.41
  42.5 0.0 copy-done.1
  42.5 162.6 %forward_backward.1 = (f32[1792,256]{1,0:T(8,128)}, f32[256,100]{1,0:T(8,128)}, f32[3,512,256]{2,1,0:T(8,128)}, f32[256,128]{1,0:T(8,128)}) custom-call(f32[2048,100]{1,0:T(8,128)} %bitcast.29, f32[408,128]{1,0:T(8,128)} %copy-done.1, f32[8,2,128]{2,1,0:T(2,128)} %copy-done, f32[4,256]{1,0:T(4,128)} %biases.1, f32[3,2,256]{2,1,0:T(2,128)} %norms.1, ...), custom_call_target="tpu_custom_call" | custom-call | tf_op jit(solution)/shard_map/forward_backward/pallas_call | solution.py:874
  205.0 38.3 %sum_and_update.1 = (f32[1,1]{1,0:T(1,128)}, f32[64,100]{1,0:T(8,128)}, f32[3,128,256]{2,1,0:T(8,128)}, f32[47,64]{1,0:T(8,128)}, f32[64,100]{1,0:T(8,128)}, /*i...) custom-call(f32[1792,256]{1,0:T(8,128)} %get-tuple-element.58.pay, ...), custom_call_target="tpu_custom_call" | custom-call | tf_op jit(solution)/shard_map/sum_and_update/pallas_call | solution.py:1136
  243.3 2.7 %hand_over.1 = (f32[1,1]{1,0:T(1,128)}, f32[64,100]{1,0:T(8,128)}, f32[3,128,256]{2,1,0:T(8,128)}, f32[47,64]{1,0:T(8,128)}, f32[64,100]{1,0:T(8,128)}, /*index=...) custom-call(f32[1,1]{1,0:T(1,128)} %get-tuple-element.62.refs_0_, ...), custom_call_target="tpu_custom_call" | custom-call | tf_op jit(solution)/shard_map/hand_over/pallas_call | solution.py:1175
  (5 shorter events, 0.0 us)
Async XLA Ops:
  4.0 3.9 %collective-permute-start.1 = (f32[408,128]{1,0:T(8,128)S(1)}, f32[408,128]{1,0:T(8,128)S(1)}, u32[]{:S(2)}, u32[]{:S(2)}) collective-permute-start(f32[408,128]{1,0:T(8,128)S(1)} %fusion), channel_id=1, source_target_pairs={{0,0},{1,8},{2,2},{3,10},{4,4},{5,12},{6,6},{7,14},{8,1},{9,9},{10... | collective-permute-start | bytes 626696 | tf_op jit(solution)/shard_map/ppermute | solution.py:48
  4.7 35.8 %collective-permute-start = (f32[1,2048,100]{1,0,2:T(1,128)}, f32[1,2048,100]{1,0,2:T(1,128)S(1)}, u32[]{:S(2)}, u32[]{:S(2)}) collective-permute-start(f32[1,2048,100]{1,0,2:T(1,128)} %param.22), channel_id=1, source_target_pairs={{0,0},{1,8},{2,2},{3,10},{4,4},{5,12},{6,6},{7,14},{8,1},{9,9},{10... | collective-permute-start | bytes 2457608 | tf_op jit(solution)/shard_map/ppermute | solution.py:48
  7.9 34.5 %copy-start.1 = (f32[408,128]{1,0:T(8,128)}, f32[408,128]{1,0:T(8,128)S(1)}, u32[]{:S(2)}) copy-start(f32[408,128]{1,0:T(8,128)S(1)} %collective-permute-done.1.refs_1_) | copy-start | bytes 626692
  39.4 0.6 copy-start

commit v4 on v3

--- a/solution.py
+++ b/solution.py
@@ -1233,7 +1233,6 @@
     label_rows = rows_dev // LANES
     picks = flat[3 * e + label_rows :].reshape(-1)[: n_rows * pairs].astype(jnp.int32)
     spread = jnp.pad(picks.reshape(n_rows, pairs), ((0, 0), (0, 8 - pairs)), constant_values=-1).reshape(1, n_rows * 8)
-    spread = jnp.pad(spread, ((0, 0), (0, -spread.shape[1] % LANES)), constant_values=-1)
     at_in = 2 * hid
     at_head = at_in + -(-feat // 8) * 8
     at_small = at_head + hid // 2

time: 247 us -> 246 us (level)
  no operation moved by 1% of the time
where the time goes in v4:
time: 246 us
  Pallas kernels  234 us (95%)
  other arithmetic  4.37 us (2%)
  local copies, waits for them, and re-layouts  3.46 us (1%)
  starting transfers between devices  2.48 us (1%)
    pallas_call x1, Pallas kernels, step_call(): pl.pallas_call(functools.partial(step_kernel, n, nb, layers, nodes, all_n...  163 us
    pallas_call x1, Pallas kernels, update_call(): pl.pallas_call(functools.partial(update_kernel, n, nb, layers, all_nodes,...  38.3 us
    pallas_call x1, Pallas kernels, fill(): pl.pallas_call(functools.partial(fill_kernel, wide, rim, chunk, parts), o...  30.3 us
  transfers between devices with their start and end apart: 2, of which 0 were waited for; matrix products, arithmetic and copies ran while one was open for 1% of the time, Pallas kernels for 12%

profile of v4, /device:TPU:0, one launch (start us, length us, event | category | flops | bytes accessed | tf_op | source)
XLA Modules:
  0.0 245.9 jit_solution(1278514762498278430)
XLA Ops:
  0.6 1.0 convert_bitcast_fusion
  1.6 0.7 convert_element_type.33
  2.3 0.7 convert_element_type.35
  3.0 0.1 copy.42
  3.1 0.1 convert_element_type.36
  3.2 0.9 fusion
  4.0 0.7 collective-permute-start.1
  4.7 1.8 collective-permute-start
  7.3 0.1 add_convert_fusion.rims
  7.3 0.6 pad_maximum_fusion.power
  7.9 0.0 collective-permute-done.1.refs_1_
  7.9 0.0 copy-start.1
  7.9 0.1 slice.25
  8.1 0.6 reshape.67.refs_7_
  8.7 30.3 %adjacency_tiles.1 = (bf16[2048,3072]{1,0:T(8,128)(2,1)}, bf16[2048,3072]{1,0:T(8,128)(2,1)}, f32[8,2,128]{2,1,0:T(2,128)S(1)}) custom-call(s32[2]{0:T(128)S(1)} %add_convert_fusion.rims, f32[128,128]{1,0:T(8,128)S(1)} %get-tuple-element.98.to_ref, f32[128,128]{1,0:T(8,128)S(1)} %get-tuple-element.97.from_ref, f32[128,128]{1,0:T(8,128)S(1)} %get-tuple-element.96.weight_ref), custom_call_target="tpu_custom_call" | custom-call | tf_op jit(solution)/shard_map/adjacency_tiles/pallas_call | solution.py:206
  39.0 0.0 copy-start
  39.0 0.6 copy-done
  39.6 0.5 slice_convert_fusion.1.refs_6_
  40.1 0.0 collective-permute-done
  40.1 1.9 copy.41
  42.1 0.0 copy-done.1
  42.1 162.6 %forward_backward.1 = (f32[1792,256]{1,0:T(8,128)}, f32[256,100]{1,0:T(8,128)}, f32[3,512,256]{2,1,0:T(8,128)}, f32[256,128]{1,0:T(8,128)}) custom-call(f32[2048,100]{1,0:T(8,128)} %bitcast.29, f32[408,128]{1,0:T(8,128)} %copy-done.1, f32[8,2,128]{2,1,0:T(2,128)} %copy-done, f32[4,256]{1,0:T(4,128)} %biases.1, f32[3,2,256]{2,1,0:T(2,128)} %norms.1, ...), custom_call_target="tpu_custom_call" | custom-call | tf_op jit(solution)/shard_map/forward_backward/pallas_call | solution.py:874
  204.7 38.3 %sum_and_update.1 = (f32[1,1]{1,0:T(1,128)}, f32[64,100]{1,0:T(8,128)}, f32[3,128,256]{2,1,0:T(8,128)}, f32[47,64]{1,0:T(8,128)}, f32[64,100]{1,0:T(8,128)}, /*i...) custom-call(f32[1792,256]{1,0:T(8,128)} %get-tuple-element.58.pay, ...), custom_call_target="tpu_custom_call" | custom-call | tf_op jit(solution)/shard_map/sum_and_update/pallas_call | solution.py:1136
  243.0 2.7 %hand_over.1 = (f32[1,1]{1,0:T(1,128)}, f32[64,100]{1,0:T(8,128)}, f32[3,128,256]{2,1,0:T(8,128)}, f32[47,64]{1,0:T(8,128)}, f32[64,100]{1,0:T(8,128)}, /*index=...) custom-call(f32[1,1]{1,0:T(1,128)} %get-tuple-element.62.refs_0_, ...), custom_call_target="tpu_custom_call" | custom-call | tf_op jit(solution)/shard_map/hand_over/pallas_call | solution.py:1175
  (5 shorter events, 0.0 us)
Async XLA Ops:
  4.0 3.9 %collective-permute-start.1 = (f32[408,128]{1,0:T(8,128)S(1)}, f32[408,128]{1,0:T(8,128)S(1)}, u32[]{:S(2)}, u32[]{:S(2)}) collective-permute-start(f32[408,128]{1,0:T(8,128)S(1)} %fusion), channel_id=1, source_target_pairs={{0,0},{1,8},{2,2},{3,10},{4,4},{5,12},{6,6},{7,14},{8,1},{9,9},{10... | collective-permute-start | bytes 626696 | tf_op jit(solution)/shard_map/ppermute | solution.py:48
  4.7 35.4 %collective-permute-start = (f32[1,2048,100]{1,0,2:T(1,128)}, f32[1,2048,100]{1,0,2:T(1,128)S(1)}, u32[]{:S(2)}, u32[]{:S(2)}) collective-permute-start(f32[1,2048,100]{1,0,2:T(1,128)} %param.22), channel_id=1, source_target_pairs={{0,0},{1,8},{2,2},{3,10},{4,4},{5,12},{6,6},{7,14},{8,1},{9,9},{10... | collective-permute-start | bytes 2457608 | tf_op jit(solution)/shard_map/ppermute | solution.py:48
  7.9 34.2 %copy-start.1 = (f32[408,128]{1,0:T(8,128)}, f32[408,128]{1,0:T(8,128)S(1)}, u32[]{:S(2)}) copy-start(f32[408,128]{1,0:T(8,128)S(1)} %collective-permute-done.1.refs_1_) | copy-start | bytes 626692
  39.0 0.6 copy-start
